TPU v7x, 256 devices: a whole 4x4x8 slice. The times are simulated.
256 devices in a mesh: outer: 16 (over z, core), inner: 16 (over y, x).
Axes of the slice: x: 4, y: 4, z: 8, core: 2. Of those that a mesh axis runs over, the one named last changes fastest.
Arguments:
- queries: bfloat16 [32768, 4096], P(('outer', 'inner')), may hold values from -48 to 48
- keys: bfloat16 [32768, 1024], P(('outer', 'inner')), may hold values from -20 to 20
- values: bfloat16 [32768, 1024], P(('outer', 'inner')), may hold values from -6 to 6
- ancestors: int32 [256, 8], replicated, may hold values from -1 to 255, as said below
- token_block: int32 [32768], replicated, may hold values from 0 to 255, as said below
- positions: int32 [32768], replicated, may hold values from 0 to 1023, as said below
Outputs:
- attended: bfloat16 [32768, 4096], P(('outer', 'inner'))
Inputs may be any that keep to these rules, and one draw needn't show every extreme that they name: `ancestors`: row b lists the blocks on the path from the root block 0 to block b, root first and b last, then -1; a parent has a smaller number than its child; some row lists 8 blocks. `token_block`: each aligned span of 128 tokens belongs to one block, and every block fills exactly one span; apart from block 0, no two blocks of one root path lie in the same aligned group of 2048 tokens. `positions`: a token's position is 128 times (the number of blocks on its block's root path minus 1) plus its offset within its span.
All inputs are finite; a program needn't handle non-finite values.
Results may differ from a plain program's by a relative error of at most 0.0065.
Values may be sent and summed in bfloat16 or wider, within the bound.
No kernel may reach another device: no remote copies, remote signals or barrier semaphores. Data moves between devices by JAX's collectives and lax.ppermute only.
A program may use at most 128 MiB of HBM per device.

v0:
```python
import functools

import jax
import jax.numpy as jnp
import numpy as np
from jax import lax
from jax.experimental import pallas as pl
from jax.experimental.pallas import tpu as pltpu
from jax.sharding import Mesh
from jax.sharding import PartitionSpec as P


HEADS = 32
KV_HEADS = 8
GROUP = HEADS // KV_HEADS
HEAD_DIM = 128
BLOCK = 128
ANC_MAX = 8
SLOTS = ANC_MAX - 1
DEVICES = 256
PLANES = 8
CAP = 34
HALF = BLOCK // 2
SHIFTS = ((0, 1, 7, 2), (6, 3, 5, 4))
GROUPS = len(SHIFTS)
STEPS = ((5, 4), (7, 3), (6, 2), (1, 0))
KV_SCRATCH = [
    pltpu.VMEM((ANC_MAX * BLOCK, HEAD_DIM), jnp.bfloat16),
    pltpu.VMEM((ANC_MAX * BLOCK, 2 * HEAD_DIM), jnp.bfloat16),
]
PACK = (GROUP + 2) * HEAD_DIM
ROTARY_BASE = 500000.0
AXES = ("z", "c", "y", "xh", "xl")
HEAD_AXES = ("y", "xl")
NEG = -1e30
EXP2_SCALE = float(HEAD_DIM**-0.5 * np.log2(np.e))

HBM = pl.BlockSpec(memory_space=pltpu.HBM)
SMEM = pl.BlockSpec(memory_space=pltpu.SMEM)
VMEM = pl.BlockSpec(memory_space=pltpu.VMEM)
VMEM_ONE = pl.BlockSpec((1, 1), lambda h: (0, 0))


def room(mib):
    return pltpu.CompilerParams(vmem_limit_bytes=mib << 20)


def inverse_row():
    half = HEAD_DIM // 2
    inv = (ROTARY_BASE ** (-2.0 * np.arange(half, dtype=np.float64) / HEAD_DIM)).astype(np.float32)
    return np.concatenate([inv, inv])[None, :]


def turn(x, cosine, sine):
    x = x.astype(jnp.float32)
    return (x * cosine + pltpu.roll(x, HEAD_DIM // 2, 1) * sine).astype(jnp.bfloat16)


def device_index():
    z, c, y, xh, xl = [lax.axis_index(name) for name in AXES]
    return (((z * 2 + c) * 4 + y) * 2 + xh) * 2 + xl


def spread_kernel(
    pos_ref, inv_ref, k_hbm, v_hbm, send_ref, cos_ref, sin_ref, own_ref, v_ref, base_ref, sems
):
    start = pl.multiple_of(device_index() * BLOCK, BLOCK)
    loads = [
        pltpu.make_async_copy(pos_ref.at[pl.ds(start, BLOCK)], base_ref, sems.at[0]),
        pltpu.make_async_copy(k_hbm, own_ref, sems.at[1]),
        pltpu.make_async_copy(v_hbm, v_ref, sems.at[2]),
    ]
    for load in loads:
        load.start()
    loads[0].wait()
    rows = lax.broadcasted_iota(jnp.int32, (BLOCK, HEAD_DIM), 0) + base_ref[0]
    lanes = lax.broadcasted_iota(jnp.int32, (BLOCK, HEAD_DIM), 1)
    angles = rows.astype(jnp.float32) * inv_ref[...]
    cosine = jnp.cos(angles)
    sine = jnp.sin(angles)
    sine = jnp.where(lanes < HEAD_DIM // 2, -sine, sine)
    cos_ref[...] = cosine
    sin_ref[...] = sine
    loads[1].wait()
    loads[2].wait()
    for h in range(KV_HEADS):
        cols = slice(h * HEAD_DIM, (h + 1) * HEAD_DIM)
        turned = turn(own_ref[:, cols], cosine, sine)
        own_ref[:, cols] = turned
        plain = v_ref[:, cols]
        for high in range(2):
            for low in range(8):
                t = (high * 8 + low) * 8
                send_ref[low, 0, h // 2, high, h % 2] = turned[t : t + 8]
                send_ref[low, 1, h // 2, high, h % 2] = plain[t : t + 8]


def bundle_kernel(count_ref, cos_ref, sin_ref, q_ref, k_ref, v_ref, out_ref):
    for g in range(GROUP):
        cols = slice(g * HEAD_DIM, (g + 1) * HEAD_DIM)
        out_ref[:, cols] = turn(q_ref[:, cols], cos_ref[...], sin_ref[...])
    out_ref[:, GROUP * HEAD_DIM : (GROUP + 1) * HEAD_DIM] = k_ref[...]
    out_ref[:, (GROUP + 1) * HEAD_DIM :] = v_ref[...]


def plan_kernel(token_ref, anc_ref, picks_ref, slots_ref, count_ref):
    n = DEVICES
    f32, bf, i32 = jnp.float32, jnp.bfloat16, jnp.int32
    across = (((1,), (1,)), ((), ()))
    anc = anc_ref[...]
    col = token_ref[:, 0:1]
    lane = lax.broadcasted_iota(i32, (n, n), 1)
    sub = lax.broadcasted_iota(i32, (n, n), 0)
    row = jnp.sum(jnp.where(sub == lane, col, 0), axis=0, keepdims=True)
    depth = jnp.sum((anc >= 0).astype(i32), axis=0, keepdims=True)
    holds = jnp.zeros((n, n), f32)
    for j in range(SLOTS):
        entry = jnp.where(j < depth - 1, anc[j : j + 1], -1)
        holds = jnp.where(entry == col, 1.0, holds)
    block_at = (col == lane).astype(f32).astype(bf)
    plane8 = lax.broadcasted_iota(i32, (PLANES, n), 0)
    lane8 = lax.broadcasted_iota(i32, (PLANES, n), 1)
    in_plane = (lane8 // (n // PLANES) == plane8).astype(f32).astype(bf)
    blocks = jnp.dot(in_plane, block_at, preferred_element_type=f32)
    need = lax.dot_general(
        blocks.astype(bf), holds.astype(bf), across, preferred_element_type=f32
    )
    needed = (need > 0.5).astype(f32)
    upto = (sub <= lane).astype(f32).astype(bf)
    ranks = jnp.dot(needed.astype(bf), upto, preferred_element_type=f32)
    count_ref[...] = jnp.max(ranks, axis=(0, 1), keepdims=True).astype(i32)
    ranks = ranks - 1.0
    wanted = lax.broadcasted_iota(i32, (CAP, n), 0).astype(f32)
    span = lax.broadcasted_iota(i32, (CAP, n), 1).astype(f32)
    for z in range(PLANES):
        hit = (ranks[z : z + 1] == wanted) & (needed[z : z + 1] > 0.5)
        picks_ref[:, z : z + 1] = jnp.sum(
            jnp.where(hit, span, 0.0), axis=1, keepdims=True
        ).astype(i32)
    z, c, xh = lax.axis_index("z"), lax.axis_index("c"), lax.axis_index("xh")
    mine = z * 32 + c * 16 + (plane8 // 2) * 4 + xh * 2 + plane8 % 2
    own_block = jnp.dot(
        (lane8 == mine).astype(f32).astype(bf), block_at, preferred_element_type=f32
    )
    path = lax.dot_general(
        own_block.astype(bf), anc.astype(f32).astype(bf), across, preferred_element_type=f32
    ).astype(i32)
    my_rank = jnp.sum(jnp.where(plane8 == z, ranks, 0.0), axis=0, keepdims=True)
    for j in range(SLOTS):
        slot = jnp.sum(
            jnp.where(path[:, j : j + 1] == row, my_rank, 0.0), axis=1, keepdims=True
        ).astype(i32)
        slots_ref[:, j : j + 1] = jnp.clip(slot, 0, CAP - 1)
    slots_ref[:, SLOTS:] = jnp.sum((path >= 0).astype(i32), axis=1, keepdims=True) - 1


def pack_kernel(picks_ref, src_ref, *out_refs):
    z = lax.axis_index("z")
    for d in range(PLANES):
        plane = lax.rem(z + d, PLANES)

        def one(k, carry):
            out_refs[d][k] = src_ref[picks_ref[k, plane]]
            return carry

        lax.fori_loop(0, CAP, one, 0, unroll=True)


def pick_kernel(idx_ref, src_ref, out_ref):
    def one(d, carry):
        for j in range(SLOTS):
            out_ref[d, j] = src_ref[idx_ref[d, j]]
        return carry

    lax.fori_loop(0, out_ref.shape[0], one, 0)


def attention(x_ref, k_ref, v_ref, alive, period, out_ref):
    k_ref[0:BLOCK] = x_ref[:, GROUP * HEAD_DIM : (GROUP + 1) * HEAD_DIM]
    v_ref[0:BLOCK, 0:HEAD_DIM] = x_ref[:, (GROUP + 1) * HEAD_DIM :]
    v_ref[:, HEAD_DIM:] = jnp.ones((k_ref.shape[0], HEAD_DIM), jnp.bfloat16)
    column = lax.broadcasted_iota(jnp.int32, (1, SLOTS * BLOCK), 1)
    bias = jnp.where((column // period) % SLOTS < alive, 0.0, NEG)
    row = lax.broadcasted_iota(jnp.int32, (BLOCK, BLOCK), 0)
    col = lax.broadcasted_iota(jnp.int32, (BLOCK, BLOCK), 1)
    for g in range(GROUP):
        cols = slice(g * HEAD_DIM, (g + 1) * HEAD_DIM)
        scores = lax.dot_general(
            x_ref[:, cols], k_ref[...], (((1,), (1,)), ((), ())), preferred_element_type=jnp.float32
        )
        near = jnp.where(col <= row, scores[:, :BLOCK], NEG)
        scores = jnp.concatenate([near, scores[:, BLOCK:] + bias], axis=1)
        top = jnp.max(scores, axis=1, keepdims=True)
        weights = jnp.exp2((scores - top) * EXP2_SCALE).astype(jnp.bfloat16)
        mixed = jnp.dot(weights, v_ref[...], preferred_element_type=jnp.float32)
        out_ref[:, cols] = (mixed[:, :HEAD_DIM] / mixed[:, HEAD_DIM:]).astype(jnp.bfloat16)


def own_member():
    return lax.axis_index("y") * 2 + lax.axis_index("xl")


def fill(k_ref, v_ref, at, slots_ref, m, here, there):
    def copy(dst_ref, parts):
        for j in range(SLOTS):
            slot = slots_ref[m, j]
            place = at + j * HALF
            for part in parts:
                size = part.shape[1]
                dst_ref[place : place + size, 0:HEAD_DIM] = part[slot]
                place += size

    core = lax.axis_index("c")

    @pl.when(core == 0)
    def _():
        copy(k_ref, here)
        copy(v_ref, there)

    @pl.when(core != 0)
    def _():
        copy(k_ref, there)
        copy(v_ref, here)


def dead_slots(alive):
    column = lax.broadcasted_iota(jnp.int32, (1, SLOTS * HALF), 1)
    return jnp.where(column // HALF < alive, 0.0, NEG)


def scored(x_ref, g, k_ref):
    q = x_ref[:, g * HEAD_DIM : (g + 1) * HEAD_DIM]
    return lax.dot_general(
        q, k_ref[...], (((1,), (1,)), ((), ())), preferred_element_type=jnp.float32
    )


def first_kernel(slots_ref, x_ref, *refs):
    here, there = refs[:GROUPS], refs[GROUPS : 2 * GROUPS]
    mix_ref, top_ref, sum_ref, k_ref, v_ref = refs[2 * GROUPS :]
    v_ref[:, HEAD_DIM:] = jnp.ones((BLOCK + SLOTS * HALF, HEAD_DIM), jnp.bfloat16)
    row = lax.broadcasted_iota(jnp.int32, (BLOCK, BLOCK), 0)
    col = lax.broadcasted_iota(jnp.int32, (BLOCK, BLOCK), 1)
    causal = col <= row

    def one(m, carry):
        fill(k_ref, v_ref, BLOCK, slots_ref, m, here, there)
        k_ref[0:BLOCK] = x_ref[m, :, GROUP * HEAD_DIM : (GROUP + 1) * HEAD_DIM]
        v_ref[0:BLOCK, 0:HEAD_DIM] = x_ref[m, :, (GROUP + 1) * HEAD_DIM :]
        bias = dead_slots(slots_ref[m, SLOTS])
        for g in range(GROUP):
            scores = scored(x_ref.at[m], g, k_ref)
            near = jnp.where(causal, scores[:, :BLOCK], NEG)
            scores = jnp.concatenate([near, scores[:, BLOCK:] + bias], axis=1)
            top = jnp.max(scores, axis=1, keepdims=True)
            weights = jnp.exp2((scores - top) * EXP2_SCALE).astype(jnp.bfloat16)
            mixed = jnp.dot(weights, v_ref[...], preferred_element_type=jnp.float32)
            mix_ref[m, g] = mixed[:, :HEAD_DIM]
            sum_ref[m, g] = mixed[:, HEAD_DIM : HEAD_DIM + 1]
            top_ref[m, g] = top
        return carry

    lax.fori_loop(0, KV_HEADS, one, 0)


def second_kernel(steps, slots_ref, x_ref, mix_ref, top_ref, sum_ref, *refs):
    here, there = refs[:GROUPS], refs[GROUPS : 2 * GROUPS]
    out_refs = refs[2 * GROUPS : 2 * GROUPS + len(steps)]
    k_refs, v_refs = refs[-2], refs[-1]
    for n, step in enumerate(steps):
        m = own_member() ^ step
        k_ref, v_ref, out_ref = k_refs.at[n], v_refs.at[n], out_refs[n]
        v_ref[:, HEAD_DIM:] = jnp.ones((SLOTS * HALF, HEAD_DIM), jnp.bfloat16)
        fill(k_ref, v_ref, 0, slots_ref, m, here, there)
    for n, step in enumerate(steps):
        m = own_member() ^ step
        k_ref, v_ref, out_ref = k_refs.at[n], v_refs.at[n], out_refs[n]
        bias = dead_slots(slots_ref[m, SLOTS])
        for g in range(GROUP):
            scores = scored(x_ref.at[m], g, k_ref) + bias
            before = top_ref[m, g]
            top = jnp.maximum(before, jnp.max(scores, axis=1, keepdims=True))
            weights = jnp.exp2((scores - top) * EXP2_SCALE).astype(jnp.bfloat16)
            mixed = jnp.dot(weights, v_ref[...], preferred_element_type=jnp.float32)
            keep = jnp.exp2((before - top) * EXP2_SCALE)
            total = mixed[:, HEAD_DIM:] + keep * sum_ref[m, g]
            mixed = mixed[:, :HEAD_DIM] + keep * mix_ref[m, g]
            out_ref[:, g * HEAD_DIM : (g + 1) * HEAD_DIM] = (mixed / total).astype(jnp.bfloat16)


def head_kernel(alive_ref, x_ref, far_k_ref, far_v_ref, out_ref, k_ref, v_ref):
    k_ref[BLOCK:] = far_k_ref[...]
    v_ref[BLOCK:, 0:HEAD_DIM] = far_v_ref[...]
    attention(x_ref, k_ref, v_ref, alive_ref[0], HALF, out_ref)


def join_kernel(*refs):
    out_ref, sems = refs[-2], refs[-1]
    width = GROUP * HEAD_DIM
    copies = []
    for step in range(KV_HEADS):
        at = pl.multiple_of((own_member() ^ step) * width, width)
        copies.append(
            pltpu.make_async_copy(refs[step], out_ref.at[:, pl.ds(at, width)], sems.at[step])
        )
    for copy in copies:
        copy.start()
    for copy in copies:
        copy.wait()


def quick(picks, slots, chunks, members):
    bf = jnp.bfloat16
    packs = pl.pallas_call(
        pack_kernel,
        out_shape=[jax.ShapeDtypeStruct((CAP, 8, HEAD_DIM), bf)] * PLANES,
        in_specs=[SMEM, VMEM],
        compiler_params=room(8),
    )(picks, chunks)
    swap = [(0, 1), (1, 0)]
    got = {0: packs[0]}
    for shifts in SHIFTS:
        for d in shifts:
            if d:
                pairs = [(i, (i + d) % PLANES) for i in range(PLANES)]
                got[d] = lax.ppermute(packs[d], "z", pairs)
    f32 = jnp.float32
    near = [
        jnp.stack([got[d] for d in shifts], axis=1).reshape(CAP, 8 * len(shifts), HEAD_DIM)
        for shifts in SHIFTS
    ]
    far, near_there = [], []
    for part in near:
        far.append(lax.ppermute(part, "xh", swap))
        near_there.append(lax.ppermute(part, "c", swap))
    keys = BLOCK + SLOTS * HALF
    running = pl.pallas_call(
        first_kernel,
        out_shape=(
            jax.ShapeDtypeStruct((KV_HEADS, GROUP, BLOCK, HEAD_DIM), f32),
            jax.ShapeDtypeStruct((KV_HEADS, GROUP, BLOCK, 1), f32),
            jax.ShapeDtypeStruct((KV_HEADS, GROUP, BLOCK, 1), f32),
        ),
        in_specs=[SMEM] + [VMEM] * (1 + 2 * GROUPS),
        out_specs=[VMEM] * 3,
        scratch_shapes=[pltpu.VMEM((keys, HEAD_DIM), bf), pltpu.VMEM((keys, 2 * HEAD_DIM), bf)],
        compiler_params=room(24),
        cost_estimate=pl.CostEstimate(flops=1 << 31, bytes_accessed=4 << 20, transcendentals=2 << 20),
    )(slots, members, *near, *near_there)
    far, running = lax.optimization_barrier((far, running))
    far_there = [lax.ppermute(part, "c", swap) for part in far]
    outs = {}
    for steps in STEPS:
        count = len(steps)
        keys = SLOTS * HALF
        results = pl.pallas_call(
            functools.partial(second_kernel, steps),
            out_shape=[jax.ShapeDtypeStruct((BLOCK, GROUP * HEAD_DIM), bf)] * count,
            in_specs=[SMEM] + [VMEM] * (4 + 2 * GROUPS),
            out_specs=[VMEM] * count,
            scratch_shapes=[
                pltpu.VMEM((count, keys, HEAD_DIM), bf),
                pltpu.VMEM((count, keys, 2 * HEAD_DIM), bf),
            ],
            compiler_params=room(24),
            cost_estimate=pl.CostEstimate(
                flops=1 << 29, bytes_accessed=1 << 20, transcendentals=1 << 19
            ),
        )(slots, members, *running, *far, *far_there)
        for step, out in zip(steps, results):
            pairs = [(m, m ^ step) for m in range(KV_HEADS)]
            outs[step] = lax.ppermute(out, HEAD_AXES, pairs) if step else out
    return [outs[step] for step in range(KV_HEADS)]


def join(outs, *unused):
    return pl.pallas_call(
        join_kernel,
        out_shape=jax.ShapeDtypeStruct((BLOCK, HEADS * HEAD_DIM), jnp.bfloat16),
        in_specs=[VMEM] * KV_HEADS,
        out_specs=HBM,
        scratch_shapes=[pltpu.SemaphoreType.DMA((KV_HEADS,))],
        compiler_params=room(8),
    )(*outs)


def general(outs, chunks, bundle, token_block, ancestors):
    bf = jnp.bfloat16
    span_blocks = token_block.reshape(DEVICES, BLOCK)[:, 0]
    ids = jnp.arange(DEVICES, dtype=jnp.int32)
    span_of = jnp.sum(jnp.where(span_blocks[:, None] == ids[None, :], ids[:, None], 0), axis=0)
    lineage = ancestors[span_blocks]
    depth = jnp.sum((lineage >= 0).astype(jnp.int32), axis=1)
    spans = span_of[jnp.maximum(lineage, 0)]
    alive = lax.dynamic_slice_in_dim(depth - 1, lax.axis_index(AXES), 1)
    packed = pl.pallas_call(
        pick_kernel,
        out_shape=jax.ShapeDtypeStruct((DEVICES, SLOTS, 8, HEAD_DIM), bf),
        in_specs=[SMEM, VMEM],
    )(spans, chunks)
    got = lax.all_to_all(packed.reshape(DEVICES, SLOTS * 8, HEAD_DIM), AXES, 0, 0, tiled=True)
    got = got.reshape(8, 2, 4, 2, 2, SLOTS, 8, HEAD_DIM).transpose(1, 2, 4, 3, 5, 0, 6, 7)
    got = got.reshape(2, KV_HEADS, SLOTS * BLOCK, HEAD_DIM)
    far_k = pl.BlockSpec((None, None, SLOTS * BLOCK, HEAD_DIM), lambda h: (0, h, 0, 0))
    far_v = pl.BlockSpec((None, None, SLOTS * BLOCK, HEAD_DIM), lambda h: (1, h, 0, 0))
    return pl.pallas_call(
        head_kernel,
        grid=(KV_HEADS,),
        out_shape=jax.ShapeDtypeStruct((BLOCK, HEADS * HEAD_DIM), bf),
        in_specs=[SMEM, pl.BlockSpec((None, BLOCK, PACK), lambda h: (h, 0, 0)), far_k, far_v],
        out_specs=pl.BlockSpec((BLOCK, GROUP * HEAD_DIM), lambda h: (0, h)),
        scratch_shapes=KV_SCRATCH,
    )(alive, bundle, got, got)


def shards(queries, keys, values, ancestors, token_block, positions):
    bf, f32, i32 = jnp.bfloat16, jnp.float32, jnp.int32
    send, cosine, sine, own_k = pl.pallas_call(
        spread_kernel,
        out_shape=(
            jax.ShapeDtypeStruct((8, 2, 4, 2, 2, 8, HEAD_DIM), bf),
            jax.ShapeDtypeStruct((BLOCK, HEAD_DIM), f32),
            jax.ShapeDtypeStruct((BLOCK, HEAD_DIM), f32),
            jax.ShapeDtypeStruct((BLOCK, KV_HEADS * HEAD_DIM), bf),
        ),
        in_specs=[HBM, VMEM, HBM, HBM],
        scratch_shapes=[
            pltpu.VMEM((BLOCK, KV_HEADS * HEAD_DIM), bf),
            pltpu.SMEM((BLOCK,), i32),
            pltpu.SemaphoreType.DMA((3,)),
        ],
    )(positions, jnp.asarray(inverse_row()), keys, values)
    chunks = lax.all_to_all(send.reshape(DEVICES, 8, HEAD_DIM), AXES, 0, 0, tiled=True)
    table = pl.BlockSpec((BLOCK, HEAD_DIM), lambda h: (0, 0))
    head = pl.BlockSpec((BLOCK, HEAD_DIM), lambda h: (0, h))
    picks, slots, count = pl.pallas_call(
        plan_kernel,
        out_shape=(
            jax.ShapeDtypeStruct((CAP, PLANES), i32),
            jax.ShapeDtypeStruct((8, ANC_MAX), i32),
            jax.ShapeDtypeStruct((1, 1), i32),
        ),
        in_specs=[VMEM, VMEM],
        compiler_params=room(8),
        cost_estimate=pl.CostEstimate(flops=4 << 20, bytes_accessed=4 << 20, transcendentals=0),
    )(token_block.reshape(DEVICES, BLOCK), ancestors.T)
    bundle = pl.pallas_call(
        bundle_kernel,
        grid=(KV_HEADS,),
        out_shape=jax.ShapeDtypeStruct((KV_HEADS, BLOCK, PACK), bf),
        in_specs=[VMEM_ONE, table, table, pl.BlockSpec((BLOCK, GROUP * HEAD_DIM), lambda h: (0, h)), head, head],
        out_specs=pl.BlockSpec((None, BLOCK, PACK), lambda h: (h, 0, 0)),
        compiler_params=room(8),
        cost_estimate=pl.CostEstimate(flops=4 << 20, bytes_accessed=4 << 20, transcendentals=0),
    )(count, cosine, sine, queries, own_k, values)
    members = lax.all_to_all(bundle, HEAD_AXES, 0, 0, tiled=True)
    fits = count[0, 0] <= CAP
    outs = quick(picks, slots, chunks, members)
    return lax.cond(fits, join, general, outs, chunks, bundle, token_block, ancestors)


def solution(mesh):
    fine = Mesh(mesh.devices.reshape(8, 2, 4, 2, 2), AXES)
    rows = P(AXES, None)

    return jax.shard_map(
        shards,
        mesh=fine,
        in_specs=(rows, rows, rows, P(), P(), P()),
        out_specs=rows,
        check_vma=False,
    )
```

profile of v0, /device:TPU:1, one launch (start us, length us, event | category | flops | bytes accessed | tf_op | source)
XLA Modules:
  0.0 114.1 jit_solution(11838502579456388085)
XLA Ops:
  0.0 2.9 %shard_map.76 = (bf16[8,2,4,2,2,8,128]{6,5,4,3,2,1,0:T(8,128)(2,1)}, f32[128,128]{1,0:T(8,128)}, f32[128,128]{1,0:T(8,128)}, bf16[128,1024]{1,0:T(8,128)(2,1)}) custom-call(s32[32768]{0:T(1024)} %pos_ref.1, f32[1,128]{1,0:T(1,128)} %constant.46.clone.inv_ref, bf16[128,1024]{1,0:T(8,128)(2,1)} %k_hbm.1, bf16[128,1024]{1,0:T(8,128)(2,1)} %v_ref.1), custom_call_target="tpu_custom_call" | custom-call | tf_op jit(solution)/shard_map/pallas_call | solution.py:418
  2.9 15.7 %all-to-all-start.1 = ((bf16[256,8,128]{2,1,0:T(8,128)(2,1)}), bf16[256,8,128]{2,1,0:T(8,128)(2,1)S(1)}, u32[]{:S(2)}, u32[]{:S(2)}) async-start(bf16[256,8,128]{2,1,0:T(8,128)(2,1)} %bitcast.26), calls=%async_computation.1 | async-start | bytes 1048576 | tf_op jit(solution)/shard_map/all_to_all | solution.py:433
  18.5 2.1 %shard_map.75 = (s32[34,8]{1,0:T(8,128)S(1)}, s32[8,8]{1,0:T(8,128)S(1)}, s32[1,1]{1,0:T(1,128)}) custom-call(s32[256,128]{1,0:T(8,128)} %bitcast.27, s32[8,256]{1,0:T(8,128)} %bitcast.36), custom_call_target="tpu_custom_call" | custom-call | flops 4194304 | bytes 4194304 | tf_op jit(solution)/shard_map/pallas_call | solution.py:436
  20.6 0.9 copy-done.1
  21.6 0.9 copy-done.2
  22.5 0.8 copy-done.3
  23.3 0.8 copy-done.4
  24.2 4.1 %shard_map.77 = bf16[8,128,768]{2,1,0:T(8,128)(2,1)} custom-call(s32[1,1]{1,0:T(1,128)} %get-tuple-element.75.count_ref, f32[128,128]{1,0:T(8,128)S(1)} %copy-done.3, f32[128,128]{1,0:T(8,128)S(1)} %copy-done.4, bf16[128,4096]{1,0:T(8,128)(2,1)S(1)} %copy-done, bf16[128,1024]{1,0:T(8,128)(2,1)S(1)} %copy-done.2, bf16[128,1024]{1,0:T(8,128)(2,1)S(1)} %copy-done.1), custom_call_target="tpu_custom_call" | custom-call | flops 4194304 | bytes 4194304 | tf_op jit(solution)/shard_map/pallas_call | solution.py:447
  28.3 11.1 %all-to-all-done.1.src_ref = bf16[256,8,128]{2,1,0:T(8,128)(2,1)S(1)} async-done(((bf16[256,8,128]{2,1,0:T(8,128)(2,1)}), bf16[256,8,128]{2,1,0:T(8,128)(2,1)S(1)}, u32[]{:S(2)}, u32[]{:S(2)}) %all-to-all-start.1) | async-done | bytes 524320 | tf_op jit(solution)/shard_map/all_to_all | solution.py:433
  39.4 3.6 %all-to-all-start.2 = ((bf16[8,128,768]{2,1,0:T(8,128)(2,1)}), bf16[8,128,768]{2,1,0:T(8,128)(2,1)S(1)}, u32[]{:S(2)}, u32[]{:S(2)}) async-start(bf16[8,128,768]{2,1,0:T(8,128)(2,1)} %shard_map.77), calls=%async_computation.2 | async-start | bytes 3145728 | tf_op jit(solution)/shard_map/all_to_all | solution.py:456
  43.0 1.3 %shard_map.78 = (bf16[34,8,128]{2,1,0:T(8,128)(2,1)S(1)}, bf16[34,8,128]{2,1,0:T(8,128)(2,1)S(1)}, bf16[34,8,128]{2,1,0:T(8,128)(2,1)S(1)}, bf16[34,8,128]{2,1,0...) custom-call(s32[34,8]{1,0:T(8,128)S(1)} %get-tuple-element.81.picks_, ...), custom_call_target="tpu_custom_call" | custom-call | tf_op jit(solution)/shard_map/pallas_call | solution.py:314
  44.2 0.1 collective-permute-start.4
  44.3 2.8 %collective-permute-start.5 = (bf16[34,8,128]{2,1,0:T(8,128)(2,1)S(1)}, bf16[34,8,128]{2,1,0:T(8,128)(2,1)S(1)}, u32[]{:S(2)}, u32[]{:S(2)}) collective-permute-start(bf16[34,8,128]{2,1,0:T(8,128)(2,1)S(1)} %get-tuple-element.87), channel_id=1, source_target_pairs={{0,96},{32,128},{64,160},{96,192},{128,224},{160,0},{192,32},{224,... | collective-permute-start | bytes 208904 | tf_op jit(solution)/shard_map/ppermute | solution.py:326
  47.1 1.8 %collective-permute-start.6 = (bf16[34,8,128]{2,1,0:T(8,128)(2,1)S(1)}, bf16[34,8,128]{2,1,0:T(8,128)(2,1)S(1)}, u32[]{:S(2)}, u32[]{:S(2)}) collective-permute-start(bf16[34,8,128]{2,1,0:T(8,128)(2,1)S(1)} %get-tuple-element.88), channel_id=1, source_target_pairs={{0,160},{32,192},{64,224},{96,0},{128,32},{160,64},{192,96},{224,1... | collective-permute-start | bytes 208904 | tf_op jit(solution)/shard_map/ppermute | solution.py:326
  48.9 4.3 %collective-permute-start.7 = (bf16[34,8,128]{2,1,0:T(8,128)(2,1)S(1)}, bf16[34,8,128]{2,1,0:T(8,128)(2,1)S(1)}, u32[]{:S(2)}, u32[]{:S(2)}) collective-permute-start(bf16[34,8,128]{2,1,0:T(8,128)(2,1)S(1)} %get-tuple-element.89), channel_id=1, source_target_pairs={{0,128},{32,160},{64,192},{96,224},{128,0},{160,32},{192,64},{224,... | collective-permute-start | bytes 208904 | tf_op jit(solution)/shard_map/ppermute | solution.py:326
  53.2 0.0 collective-permute-start
  53.2 0.0 collective-permute-done.4
  53.2 2.7 %collective-permute-start.1 = (bf16[34,8,128]{2,1,0:T(8,128)(2,1)S(1)}, bf16[34,8,128]{2,1,0:T(8,128)(2,1)S(1)}, u32[]{:S(2)}, u32[]{:S(2)}) collective-permute-start(bf16[34,8,128]{2,1,0:T(8,128)(2,1)S(1)} %get-tuple-element.84), channel_id=1, source_target_pairs={{0,224},{32,0},{64,32},{96,64},{128,96},{160,128},{192,160},{224,1... | collective-permute-start | bytes 208904 | tf_op jit(solution)/shard_map/ppermute | solution.py:326
  55.8 0.0 collective-permute-done.5
  55.8 0.0 collective-permute-start.2
  55.9 0.0 collective-permute-done.6
  55.9 1.5 %collective-permute-done.7 = bf16[34,8,128]{2,1,0:T(8,128)(2,1)S(1)} collective-permute-done((bf16[34,8,128]{2,1,0:T(8,128)(2,1)S(1)}, bf16[34,8,128]{2,1,0:T(8,128)(2,1)S(1)}, u32[]{:S(2)}, u32[]{:S(2)}) %collective-permute-start.7) | collective-permute-done | bytes 69664 | tf_op jit(solution)/shard_map/ppermute | solution.py:326
  57.4 3.0 %collective-permute-start.10 = (bf16[34,32,128]{2,1,0:T(8,128)(2,1)S(1)}, bf16[34,32,128]{2,1,0:T(8,128)(2,1)S(1)}, u32[]{:S(2)}, u32[]{:S(2)}) collective-permute-start(bf16[34,32,128]{2,1,0:T(8,128)(2,1)S(1)} %copy_bitcast_fusion.refs_1_), channel_id=1, source_target_pairs={{0,16},{16,0},{1,17},{17,1},{2,18},{18,2},{3,19},{19,3},{4,20},{20... | collective-permute-start | bytes 835592 | tf_op jit(solution)/shard_map/ppermute | solution.py:335
  60.4 0.0 collective-permute-done
  60.4 0.0 collective-permute-done.1
  60.4 1.4 %collective-permute-done.2 = bf16[34,8,128]{2,1,0:T(8,128)(2,1)S(1)} collective-permute-done((bf16[34,8,128]{2,1,0:T(8,128)(2,1)S(1)}, bf16[34,8,128]{2,1,0:T(8,128)(2,1)S(1)}, u32[]{:S(2)}, u32[]{:S(2)}) %collective-permute-start.2) | collective-permute-done | bytes 69664 | tf_op jit(solution)/shard_map/ppermute | solution.py:326
  61.9 2.5 %collective-permute-start.9 = (bf16[34,32,128]{2,1,0:T(8,128)(2,1)S(1)}, bf16[34,32,128]{2,1,0:T(8,128)(2,1)S(1)}, u32[]{:S(2)}, u32[]{:S(2)}) collective-permute-start(bf16[34,32,128]{2,1,0:T(8,128)(2,1)S(1)} %copy_bitcast_fusion.1.refs_0_), channel_id=1, source_target_pairs={{0,16},{16,0},{1,17},{17,1},{2,18},{18,2},{3,19},{19,3},{4,20},{20... | collective-permute-start | bytes 835592 | tf_op jit(solution)/shard_map/ppermute | solution.py:335
  64.4 1.4 %collective-permute-start.8 = (bf16[34,32,128]{2,1,0:T(8,128)(2,1)S(1)}, bf16[34,32,128]{2,1,0:T(8,128)(2,1)S(1)}, u32[]{:S(2)}, u32[]{:S(2)}) collective-permute-start(bf16[34,32,128]{2,1,0:T(8,128)(2,1)S(1)} %copy_bitcast_fusion.refs_1_), channel_id=1, source_target_pairs={{0,2},{2,0},{1,3},{3,1},{4,6},{6,4},{5,7},{7,5},{8,10},{10,8},{9,1... | collective-permute-start | bytes 835592 | tf_op jit(solution)/shard_map/ppermute | solution.py:334
  65.7 1.6 %collective-permute-start.3 = (bf16[34,32,128]{2,1,0:T(8,128)(2,1)S(1)}, bf16[34,32,128]{2,1,0:T(8,128)(2,1)S(1)}, u32[]{:S(2)}, u32[]{:S(2)}) collective-permute-start(bf16[34,32,128]{2,1,0:T(8,128)(2,1)S(1)} %copy_bitcast_fusion.1.refs_0_), channel_id=1, source_target_pairs={{0,2},{2,0},{1,3},{3,1},{4,6},{6,4},{5,7},{7,5},{8,10},{10,8},{9,1... | collective-permute-start | bytes 835592 | tf_op jit(solution)/shard_map/ppermute | solution.py:334
  67.3 0.0 all-to-all-done.2.x_ref
  67.3 0.0 collective-permute-done.10.refs_3_
  67.3 0.0 collective-permute-done.9.refs_2_
  67.3 8.3 %shard_map.79 = (f32[8,4,128,128]{3,2,1,0:T(8,128)S(1)}, f32[8,4,128,1]{3,2,1,0:T(8,128)S(1)}, f32[8,4,128,1]{3,2,1,0:T(8,128)S(1)}) custom-call(s32[8,8]{1,0:T(8,128)S(1)} %get-tuple-element.80.slots_ref, bf16[8,128,768]{2,1,0:T(8,128)(2,1)S(1)} %all-to-all-done.2.x_ref, bf16[34,32,128]{2,1,0:T(8,128)(2,1)S(1)} %copy_bitcast_fusion.1.refs_0_, ...), custom_call_target="tpu_custom_call" | custom-call | flops 2147483648 | bytes 4194304 | tf_op jit(solution)/shard_map/pallas_call | solution.py:337
  75.7 0.0 collective-permute-done.8.refs_1_
  75.7 4.2 %collective-permute-done.3.refs_0_ = bf16[34,32,128]{2,1,0:T(8,128)(2,1)S(1)} collective-permute-done((bf16[34,32,128]{2,1,0:T(8,128)(2,1)S(1)}, bf16[34,32,128]{2,1,0:T(8,128)(2,1)S(1)}, u32[]{:S(2)}, u32[]{:S(2)}) %collective-permute-start.3) | collective-permute-done | bytes 278560 | tf_op jit(solution)/shard_map/ppermute | solution.py:334
  80.0 1.0 collective-permute-start.11
  80.9 0.0 collective-permute-start.12
  80.9 1.2 %collective-permute-done.11.refs_2_ = bf16[34,32,128]{2,1,0:T(8,128)(2,1)S(1)} collective-permute-done((bf16[34,32,128]{2,1,0:T(8,128)(2,1)S(1)}, bf16[34,32,128]{2,1,0:T(8,128)(2,1)S(1)}, u32[]{:S(2)}, u32[]{:S(2)}) %collective-permute-start.11) | collective-permute-done | bytes 278560 | tf_op jit(solution)/shard_map/ppermute | solution.py:351
  82.1 0.4 collective-permute-done.12.refs_3_
  82.5 3.6 %shard_map.83 = (bf16[128,512]{1,0:T(8,128)(2,1)S(1)}, bf16[128,512]{1,0:T(8,128)(2,1)S(1)}) custom-call(s32[8,8]{1,0:T(8,128)S(1)} %get-tuple-element.80.slots_ref, bf16[8,128,768]{2,1,0:T(8,128)(2,1)S(1)} %all-to-all-done.2.x_ref, f32[8,4,128,128]{3,2,1,0:T(8,128)S(1)} %get-tuple-element.93.mix_ref, f32[8,4,128,1]{3,2,1,0:T(8,128)S(1)} %get-tuple-element.94.top_ref, ...), custom_call_target="tpu_custom_call" | custom-call | flops 536870912 | bytes 1048576 | tf_op jit(solution)/shard_map/pallas_call | solution.py:356
  86.1 3.4 %collective-permute-start.16 = (bf16[128,512]{1,0:T(8,128)(2,1)S(1)}, bf16[128,512]{1,0:T(8,128)(2,1)S(1)}, u32[]{:S(2)}, u32[]{:S(2)}) collective-permute-start(bf16[128,512]{1,0:T(8,128)(2,1)S(1)} %get-tuple-element.102), channel_id=1, source_target_pairs={{0,8},{1,9},{4,12},{5,13},{8,0},{9,1},{12,4},{13,5},{2,10},{3,11},... | collective-permute-start | bytes 393224 | tf_op jit(solution)/shard_map/ppermute | solution.py:372
  89.5 1.2 %collective-permute-start.17 = (bf16[128,512]{1,0:T(8,128)(2,1)S(1)}, bf16[128,512]{1,0:T(8,128)(2,1)S(1)}, u32[]{:S(2)}, u32[]{:S(2)}) collective-permute-start(bf16[128,512]{1,0:T(8,128)(2,1)S(1)} %get-tuple-element.103), channel_id=1, source_target_pairs={{0,9},{1,8},{4,13},{5,12},{8,1},{9,0},{12,5},{13,4},{2,11},{3,10},... | collective-permute-start | bytes 393224 | tf_op jit(solution)/shard_map/ppermute | solution.py:372
  90.7 3.6 %shard_map.82 = (bf16[128,512]{1,0:T(8,128)(2,1)S(1)}, bf16[128,512]{1,0:T(8,128)(2,1)S(1)}) custom-call(s32[8,8]{1,0:T(8,128)S(1)} %get-tuple-element.80.slots_ref, bf16[8,128,768]{2,1,0:T(8,128)(2,1)S(1)} %all-to-all-done.2.x_ref, f32[8,4,128,128]{3,2,1,0:T(8,128)S(1)} %get-tuple-element.93.mix_ref, f32[8,4,128,1]{3,2,1,0:T(8,128)S(1)} %get-tuple-element.94.top_ref, ...), custom_call_target="tpu_custom_call" | custom-call | flops 536870912 | bytes 1048576 | tf_op jit(solution)/shard_map/pallas_call | solution.py:356
  94.3 1.3 %collective-permute-start.15 = (bf16[128,512]{1,0:T(8,128)(2,1)S(1)}, bf16[128,512]{1,0:T(8,128)(2,1)S(1)}, u32[]{:S(2)}, u32[]{:S(2)}) collective-permute-start(bf16[128,512]{1,0:T(8,128)(2,1)S(1)} %get-tuple-element.101), channel_id=1, source_target_pairs={{0,5},{1,4},{4,1},{5,0},{8,13},{9,12},{12,9},{13,8},{2,7},{3,6},{6... | collective-permute-start | bytes 393224 | tf_op jit(solution)/shard_map/ppermute | solution.py:372
  95.6 2.7 %collective-permute-start.19 = (bf16[128,512]{1,0:T(8,128)(2,1)S(1)}, bf16[128,512]{1,0:T(8,128)(2,1)S(1)}, u32[]{:S(2)}, u32[]{:S(2)}) collective-permute-start(bf16[128,512]{1,0:T(8,128)(2,1)S(1)} %get-tuple-element.105), channel_id=1, source_target_pairs={{0,13},{1,12},{4,9},{5,8},{8,5},{9,4},{12,1},{13,0},{2,15},{3,14},... | collective-permute-start | bytes 393224 | tf_op jit(solution)/shard_map/ppermute | solution.py:372
  98.3 3.6 %shard_map.81 = (bf16[128,512]{1,0:T(8,128)(2,1)S(1)}, bf16[128,512]{1,0:T(8,128)(2,1)S(1)}) custom-call(s32[8,8]{1,0:T(8,128)S(1)} %get-tuple-element.80.slots_ref, bf16[8,128,768]{2,1,0:T(8,128)(2,1)S(1)} %all-to-all-done.2.x_ref, f32[8,4,128,128]{3,2,1,0:T(8,128)S(1)} %get-tuple-element.93.mix_ref, f32[8,4,128,1]{3,2,1,0:T(8,128)S(1)} %get-tuple-element.94.top_ref, ...), custom_call_target="tpu_custom_call" | custom-call | flops 536870912 | bytes 1048576 | tf_op jit(solution)/shard_map/pallas_call | solution.py:356
  102.0 0.0 copy-start.6
  102.0 0.0 copy-start.8
  102.0 0.0 copy-start.9
  102.0 0.4 collective-permute-start.14
  102.4 4.3 %shard_map.80 = (bf16[128,512]{1,0:T(8,128)(2,1)S(1)}, bf16[128,512]{1,0:T(8,128)(2,1)}) custom-call(s32[8,8]{1,0:T(8,128)S(1)} %get-tuple-element.80.slots_ref, bf16[8,128,768]{2,1,0:T(8,128)(2,1)S(1)} %all-to-all-done.2.x_ref, f32[8,4,128,128]{3,2,1,0:T(8,128)S(1)} %get-tuple-element.93.mix_ref, f32[8,4,128,1]{3,2,1,0:T(8,128)S(1)} %get-tuple-element.94.top_ref, ...), custom_call_target="tpu_custom_call" | custom-call | flops 536870912 | bytes 1048576 | tf_op jit(solution)/shard_map/pallas_call | solution.py:356
  106.7 0.0 collective-permute-done.16
  106.7 0.6 collective-permute-start.18
  107.3 0.0 collective-permute-done.17
  107.3 0.3 collective-permute-start.13
  108.1 0.0 collective-permute-done.15
  108.1 0.0 collective-permute-done.19
  108.1 0.0 collective-permute-done.14
  108.2 3.5 %collective-permute-done.18 = bf16[128,512]{1,0:T(8,128)(2,1)S(1)} collective-permute-done((bf16[128,512]{1,0:T(8,128)(2,1)S(1)}, bf16[128,512]{1,0:T(8,128)(2,1)S(1)}, u32[]{:S(2)}, u32[]{:S(2)}) %collective-permute-start.18) | collective-permute-done | bytes 131104 | tf_op jit(solution)/shard_map/ppermute | solution.py:372
  111.7 0.0 collective-permute-done.13
  111.7 1.4 %conditional.1 = (bf16[128,4096]{1,0:T(8,128)(2,1)S(1)}) conditional(s32[]{:T(128)} %bitcast.8, (s32[32768]{0:T(1024)S(1)}, s32[256,8]{0,1:T(8,128)S(1)}, bf16[256,8,128]{2,1,0:T(8,128)(2,1)S(1)}, bf16[8,128,768]{2,1,0:T(8,128)(2,1)}) %tuple.28, (bf16[128,512]{1,0:T(8,128)(2,1)}, bf16[128,512]{1,0:T(8,128)(2,1)S(1)}, bf16[128,512]{1,0:T(8,128)(2,1)S(1)}, ...), branch_computations={%region_0.3_spmd, %region_3.4_spmd} | conditional | flops 208409 | bytes 18487626 | solution.py:459
  112.0 1.1 branch_1_fun.1
  113.1 0.0 copy-start.7
  113.1 1.0 copy-done.7
  (13 shorter events, 0.1 us)
Async XLA Ops:
  0.0 20.6 %copy-start = (bf16[128,4096]{1,0:T(8,128)(2,1)S(1)}, bf16[128,4096]{1,0:T(8,128)(2,1)}, u32[]{:S(2)}) copy-start(bf16[128,4096]{1,0:T(8,128)(2,1)} %q_ref.1) | copy-start | bytes 3145732
  2.9 36.5 %all-to-all-start.1 = ((bf16[256,8,128]{2,1,0:T(8,128)(2,1)}), bf16[256,8,128]{2,1,0:T(8,128)(2,1)S(1)}, u32[]{:S(2)}, u32[]{:S(2)}) async-start(bf16[256,8,128]{2,1,0:T(8,128)(2,1)} %bitcast.26), calls=%async_computation.1 | async-start | bytes 1048576 | tf_op jit(solution)/shard_map/all_to_all | solution.py:433
  20.6 1.0 copy-start.1
  21.6 0.9 copy-start.2
  22.5 0.8 copy-start.3
  23.3 0.8 copy-start.4
  39.4 18.1 %copy-start.5 = (bf16[256,8,128]{2,1,0:T(8,128)(2,1)}, bf16[256,8,128]{2,1,0:T(8,128)(2,1)S(1)}, u32[]{:S(2)}) copy-start(bf16[256,8,128]{2,1,0:T(8,128)(2,1)S(1)} %all-to-all-done.1.src_ref) | copy-start | bytes 1572868
  39.4 28.0 %all-to-all-start.2 = ((bf16[8,128,768]{2,1,0:T(8,128)(2,1)}), bf16[8,128,768]{2,1,0:T(8,128)(2,1)S(1)}, u32[]{:S(2)}, u32[]{:S(2)}) async-start(bf16[8,128,768]{2,1,0:T(8,128)(2,1)} %shard_map.77), calls=%async_computation.2 | async-start | bytes 3145728 | tf_op jit(solution)/shard_map/all_to_all | solution.py:456
  44.2 9.0 %collective-permute-start.4 = (bf16[34,8,128]{2,1,0:T(8,128)(2,1)S(1)}, bf16[34,8,128]{2,1,0:T(8,128)(2,1)S(1)}, u32[]{:S(2)}, u32[]{:S(2)}) collective-permute-start(bf16[34,8,128]{2,1,0:T(8,128)(2,1)S(1)} %get-tuple-element.86), channel_id=1, source_target_pairs={{0,192},{32,224},{64,0},{96,32},{128,64},{160,96},{192,128},{224,1... | collective-permute-start | bytes 208904 | tf_op jit(solution)/shard_map/ppermute | solution.py:326
  44.3 11.5 %collective-permute-start.5 = (bf16[34,8,128]{2,1,0:T(8,128)(2,1)S(1)}, bf16[34,8,128]{2,1,0:T(8,128)(2,1)S(1)}, u32[]{:S(2)}, u32[]{:S(2)}) collective-permute-start(bf16[34,8,128]{2,1,0:T(8,128)(2,1)S(1)} %get-tuple-element.87), channel_id=1, source_target_pairs={{0,96},{32,128},{64,160},{96,192},{128,224},{160,0},{192,32},{224,... | collective-permute-start | bytes 208904 | tf_op jit(solution)/shard_map/ppermute | solution.py:326
  47.1 8.8 %collective-permute-start.6 = (bf16[34,8,128]{2,1,0:T(8,128)(2,1)S(1)}, bf16[34,8,128]{2,1,0:T(8,128)(2,1)S(1)}, u32[]{:S(2)}, u32[]{:S(2)}) collective-permute-start(bf16[34,8,128]{2,1,0:T(8,128)(2,1)S(1)} %get-tuple-element.88), channel_id=1, source_target_pairs={{0,160},{32,192},{64,224},{96,0},{128,32},{160,64},{192,96},{224,1... | collective-permute-start | bytes 208904 | tf_op jit(solution)/shard_map/ppermute | solution.py:326
  48.9 8.5 %collective-permute-start.7 = (bf16[34,8,128]{2,1,0:T(8,128)(2,1)S(1)}, bf16[34,8,128]{2,1,0:T(8,128)(2,1)S(1)}, u32[]{:S(2)}, u32[]{:S(2)}) collective-permute-start(bf16[34,8,128]{2,1,0:T(8,128)(2,1)S(1)} %get-tuple-element.89), channel_id=1, source_target_pairs={{0,128},{32,160},{64,192},{96,224},{128,0},{160,32},{192,64},{224,... | collective-permute-start | bytes 208904 | tf_op jit(solution)/shard_map/ppermute | solution.py:326
  53.2 7.3 %collective-permute-start = (bf16[34,8,128]{2,1,0:T(8,128)(2,1)S(1)}, bf16[34,8,128]{2,1,0:T(8,128)(2,1)S(1)}, u32[]{:S(2)}, u32[]{:S(2)}) collective-permute-start(bf16[34,8,128]{2,1,0:T(8,128)(2,1)S(1)} %get-tuple-element.83), channel_id=1, source_target_pairs={{0,32},{32,64},{64,96},{96,128},{128,160},{160,192},{192,224},{224... | collective-permute-start | bytes 208904 | tf_op jit(solution)/shard_map/ppermute | solution.py:326
  53.2 7.2 %collective-permute-start.1 = (bf16[34,8,128]{2,1,0:T(8,128)(2,1)S(1)}, bf16[34,8,128]{2,1,0:T(8,128)(2,1)S(1)}, u32[]{:S(2)}, u32[]{:S(2)}) collective-permute-start(bf16[34,8,128]{2,1,0:T(8,128)(2,1)S(1)} %get-tuple-element.84), channel_id=1, source_target_pairs={{0,224},{32,0},{64,32},{96,64},{128,96},{160,128},{192,160},{224,1... | collective-permute-start | bytes 208904 | tf_op jit(solution)/shard_map/ppermute | solution.py:326
  55.8 6.0 %collective-permute-start.2 = (bf16[34,8,128]{2,1,0:T(8,128)(2,1)S(1)}, bf16[34,8,128]{2,1,0:T(8,128)(2,1)S(1)}, u32[]{:S(2)}, u32[]{:S(2)}) collective-permute-start(bf16[34,8,128]{2,1,0:T(8,128)(2,1)S(1)} %get-tuple-element.85), channel_id=1, source_target_pairs={{0,64},{32,96},{64,128},{96,160},{128,192},{160,224},{192,0},{224,... | collective-permute-start | bytes 208904 | tf_op jit(solution)/shard_map/ppermute | solution.py:326
  57.4 9.9 %collective-permute-start.10 = (bf16[34,32,128]{2,1,0:T(8,128)(2,1)S(1)}, bf16[34,32,128]{2,1,0:T(8,128)(2,1)S(1)}, u32[]{:S(2)}, u32[]{:S(2)}) collective-permute-start(bf16[34,32,128]{2,1,0:T(8,128)(2,1)S(1)} %copy_bitcast_fusion.refs_1_), channel_id=1, source_target_pairs={{0,16},{16,0},{1,17},{17,1},{2,18},{18,2},{3,19},{19,3},{4,20},{20... | collective-permute-start | bytes 835592 | tf_op jit(solution)/shard_map/ppermute | solution.py:335
  61.9 5.5 %collective-permute-start.9 = (bf16[34,32,128]{2,1,0:T(8,128)(2,1)S(1)}, bf16[34,32,128]{2,1,0:T(8,128)(2,1)S(1)}, u32[]{:S(2)}, u32[]{:S(2)}) collective-permute-start(bf16[34,32,128]{2,1,0:T(8,128)(2,1)S(1)} %copy_bitcast_fusion.1.refs_0_), channel_id=1, source_target_pairs={{0,16},{16,0},{1,17},{17,1},{2,18},{18,2},{3,19},{19,3},{4,20},{20... | collective-permute-start | bytes 835592 | tf_op jit(solution)/shard_map/ppermute | solution.py:335
  64.4 11.3 %collective-permute-start.8 = (bf16[34,32,128]{2,1,0:T(8,128)(2,1)S(1)}, bf16[34,32,128]{2,1,0:T(8,128)(2,1)S(1)}, u32[]{:S(2)}, u32[]{:S(2)}) collective-permute-start(bf16[34,32,128]{2,1,0:T(8,128)(2,1)S(1)} %copy_bitcast_fusion.refs_1_), channel_id=1, source_target_pairs={{0,2},{2,0},{1,3},{3,1},{4,6},{6,4},{5,7},{7,5},{8,10},{10,8},{9,1... | collective-permute-start | bytes 835592 | tf_op jit(solution)/shard_map/ppermute | solution.py:334
  65.7 14.2 %collective-permute-start.3 = (bf16[34,32,128]{2,1,0:T(8,128)(2,1)S(1)}, bf16[34,32,128]{2,1,0:T(8,128)(2,1)S(1)}, u32[]{:S(2)}, u32[]{:S(2)}) collective-permute-start(bf16[34,32,128]{2,1,0:T(8,128)(2,1)S(1)} %copy_bitcast_fusion.1.refs_0_), channel_id=1, source_target_pairs={{0,2},{2,0},{1,3},{3,1},{4,6},{6,4},{5,7},{7,5},{8,10},{10,8},{9,1... | collective-permute-start | bytes 835592 | tf_op jit(solution)/shard_map/ppermute | solution.py:334
  80.0 2.1 %collective-permute-start.11 = (bf16[34,32,128]{2,1,0:T(8,128)(2,1)S(1)}, bf16[34,32,128]{2,1,0:T(8,128)(2,1)S(1)}, u32[]{:S(2)}, u32[]{:S(2)}) collective-permute-start(bf16[34,32,128]{2,1,0:T(8,128)(2,1)S(1)} %collective-permute-done.3.refs_0_), channel_id=1, source_target_pairs={{0,16},{16,0},{1,17},{17,1},{2,18},{18,2},{3,19},{19,3},{4,20},{20... | collective-permute-start | bytes 835592 | tf_op jit(solution)/shard_map/ppermute | solution.py:351
  80.9 1.6 %collective-permute-start.12 = (bf16[34,32,128]{2,1,0:T(8,128)(2,1)S(1)}, bf16[34,32,128]{2,1,0:T(8,128)(2,1)S(1)}, u32[]{:S(2)}, u32[]{:S(2)}) collective-permute-start(bf16[34,32,128]{2,1,0:T(8,128)(2,1)S(1)} %collective-permute-done.8.refs_1_), channel_id=1, source_target_pairs={{0,16},{16,0},{1,17},{17,1},{2,18},{18,2},{3,19},{19,3},{4,20},{20... | collective-permute-start | bytes 835592 | tf_op jit(solution)/shard_map/ppermute | solution.py:351
  86.1 20.5 %collective-permute-start.16 = (bf16[128,512]{1,0:T(8,128)(2,1)S(1)}, bf16[128,512]{1,0:T(8,128)(2,1)S(1)}, u32[]{:S(2)}, u32[]{:S(2)}) collective-permute-start(bf16[128,512]{1,0:T(8,128)(2,1)S(1)} %get-tuple-element.102), channel_id=1, source_target_pairs={{0,8},{1,9},{4,12},{5,13},{8,0},{9,1},{12,4},{13,5},{2,10},{3,11},... | collective-permute-start | bytes 393224 | tf_op jit(solution)/shard_map/ppermute | solution.py:372
  89.5 17.8 %collective-permute-start.17 = (bf16[128,512]{1,0:T(8,128)(2,1)S(1)}, bf16[128,512]{1,0:T(8,128)(2,1)S(1)}, u32[]{:S(2)}, u32[]{:S(2)}) collective-permute-start(bf16[128,512]{1,0:T(8,128)(2,1)S(1)} %get-tuple-element.103), channel_id=1, source_target_pairs={{0,9},{1,8},{4,13},{5,12},{8,1},{9,0},{12,5},{13,4},{2,11},{3,10},... | collective-permute-start | bytes 393224 | tf_op jit(solution)/shard_map/ppermute | solution.py:372
  94.3 13.8 %collective-permute-start.15 = (bf16[128,512]{1,0:T(8,128)(2,1)S(1)}, bf16[128,512]{1,0:T(8,128)(2,1)S(1)}, u32[]{:S(2)}, u32[]{:S(2)}) collective-permute-start(bf16[128,512]{1,0:T(8,128)(2,1)S(1)} %get-tuple-element.101), channel_id=1, source_target_pairs={{0,5},{1,4},{4,1},{5,0},{8,13},{9,12},{12,9},{13,8},{2,7},{3,6},{6... | collective-permute-start | bytes 393224 | tf_op jit(solution)/shard_map/ppermute | solution.py:372
  95.6 12.5 %collective-permute-start.19 = (bf16[128,512]{1,0:T(8,128)(2,1)S(1)}, bf16[128,512]{1,0:T(8,128)(2,1)S(1)}, u32[]{:S(2)}, u32[]{:S(2)}) collective-permute-start(bf16[128,512]{1,0:T(8,128)(2,1)S(1)} %get-tuple-element.105), channel_id=1, source_target_pairs={{0,13},{1,12},{4,9},{5,8},{8,5},{9,4},{12,1},{13,0},{2,15},{3,14},... | collective-permute-start | bytes 393224 | tf_op jit(solution)/shard_map/ppermute | solution.py:372
  102.0 9.7 %copy-start.6 = (bf16[256,8,128]{2,1,0:T(8,128)(2,1)S(1)}, bf16[256,8,128]{2,1,0:T(8,128)(2,1)}, u32[]{:S(2)}) copy-start(bf16[256,8,128]{2,1,0:T(8,128)(2,1)} %copy-done.5) | copy-start | bytes 1572868
  102.0 9.7 %copy-start.8 = (s32[32768]{0:T(1024)S(1)}, s32[32768]{0:T(1024)}, u32[]{:S(2)}) copy-start(s32[32768]{0:T(1024)} %param.13) | copy-start | bytes 393220
  102.0 9.7 %copy-start.9 = (s32[256,8]{0,1:T(8,128)S(1)}, s32[256,8]{0,1:T(8,128)}, u32[]{:S(2)}) copy-start(s32[256,8]{0,1:T(8,128)} %param.12) | copy-start | bytes 24580
  102.0 6.2 %collective-permute-start.14 = (bf16[128,512]{1,0:T(8,128)(2,1)S(1)}, bf16[128,512]{1,0:T(8,128)(2,1)S(1)}, u32[]{:S(2)}, u32[]{:S(2)}) collective-permute-start(bf16[128,512]{1,0:T(8,128)(2,1)S(1)} %get-tuple-element.100), channel_id=1, source_target_pairs={{0,4},{1,5},{4,0},{5,1},{8,12},{9,13},{12,8},{13,9},{2,6},{3,7},{6... | collective-permute-start | bytes 393224 | tf_op jit(solution)/shard_map/ppermute | solution.py:372
  106.7 5.0 %collective-permute-start.18 = (bf16[128,512]{1,0:T(8,128)(2,1)S(1)}, bf16[128,512]{1,0:T(8,128)(2,1)S(1)}, u32[]{:S(2)}, u32[]{:S(2)}) collective-permute-start(bf16[128,512]{1,0:T(8,128)(2,1)S(1)} %get-tuple-element.104), channel_id=1, source_target_pairs={{0,12},{1,13},{4,8},{5,9},{8,4},{9,5},{12,0},{13,1},{2,14},{3,15},... | collective-permute-start | bytes 393224 | tf_op jit(solution)/shard_map/ppermute | solution.py:372
  107.3 4.4 %collective-permute-start.13 = (bf16[128,512]{1,0:T(8,128)(2,1)S(1)}, bf16[128,512]{1,0:T(8,128)(2,1)S(1)}, u32[]{:S(2)}, u32[]{:S(2)}) collective-permute-start(bf16[128,512]{1,0:T(8,128)(2,1)S(1)} %get-tuple-element.99), channel_id=1, source_target_pairs={{0,1},{1,0},{4,5},{5,4},{8,9},{9,8},{12,13},{13,12},{2,3},{3,2},{6... | collective-permute-start | bytes 393224 | tf_op jit(solution)/shard_map/ppermute | solution.py:372
  113.1 1.0 copy-start.7
where the time goes:
time: 115 us; the launch traced here: 114 us
  starting transfers between devices  50 us (43%)
  Pallas kernels  34.9 us (30%)
  waiting for transfers between devices  23.4 us (20%)
  local copies, waits for them, and re-layouts  4.57 us (4%)
    all_to_all x1, starting transfers between devices, shards(): lax.all_to_all(send.reshape(DEVICES, 8, HEAD_DIM), AXES, 0, 0, tiled=True)  15.7 us
    pallas_call x4, Pallas kernels, quick(): pl.pallas_call(functools.partial(second_kernel, steps), out_shape=[jax.Sh...  15.2 us
    ppermute x7, starting transfers between devices, quick(): got[d] = lax.ppermute(packs[d], 'z', pairs)  11.6 us
    all_to_all x1, waiting for transfers between devices, shards(): lax.all_to_all(send.reshape(DEVICES, 8, HEAD_DIM), AXES, 0, 0, tiled=True)  11.1 us
    ppermute x7, starting transfers between devices, quick(): outs[step] = lax.ppermute(out, HEAD_AXES, pairs) if step else out  9.77 us
    pallas_call x1, Pallas kernels, quick(): pl.pallas_call(first_kernel, out_shape=(jax.ShapeDtypeStruct((KV_HEADS, G...  8.34 us
    ppermute x2, starting transfers between devices, quick(): near_there.append(lax.ppermute(part, 'c', swap))  5.47 us
    unnamed x20, local copies, waits for them, and re-layouts  4.57 us
  transfers between devices with their start and end apart: 22, of which 7 were waited for; matrix products, arithmetic and copies ran while one was open for 0% of the time, Pallas kernels for 24%

commit v1 on v0

--- a/solution.py
+++ b/solution.py
@@ -23,7 +23,6 @@
 HALF = BLOCK // 2
 SHIFTS = ((0, 1, 7, 2), (6, 3, 5, 4))
 GROUPS = len(SHIFTS)
-STEPS = ((5, 4), (7, 3), (6, 2), (1, 0))
 KV_SCRATCH = [
     pltpu.VMEM((ANC_MAX * BLOCK, HEAD_DIM), jnp.bfloat16),
     pltpu.VMEM((ANC_MAX * BLOCK, 2 * HEAD_DIM), jnp.bfloat16),
@@ -263,18 +262,14 @@
     lax.fori_loop(0, KV_HEADS, one, 0)
 
 
-def second_kernel(steps, slots_ref, x_ref, mix_ref, top_ref, sum_ref, *refs):
+def second_kernel(mask, slots_ref, x_ref, mix_ref, top_ref, sum_ref, *refs):
     here, there = refs[:GROUPS], refs[GROUPS : 2 * GROUPS]
-    out_refs = refs[2 * GROUPS : 2 * GROUPS + len(steps)]
-    k_refs, v_refs = refs[-2], refs[-1]
-    for n, step in enumerate(steps):
-        m = own_member() ^ step
-        k_ref, v_ref, out_ref = k_refs.at[n], v_refs.at[n], out_refs[n]
-        v_ref[:, HEAD_DIM:] = jnp.ones((SLOTS * HALF, HEAD_DIM), jnp.bfloat16)
+    out_refs, (k_ref, v_ref, done_ref) = refs[2 * GROUPS : -3], refs[-3:]
+    v_ref[:, HEAD_DIM:] = jnp.ones((SLOTS * HALF, HEAD_DIM), jnp.bfloat16)
+
+    def one(n, carry):
+        m = own_member() ^ mask ^ n
         fill(k_ref, v_ref, 0, slots_ref, m, here, there)
-    for n, step in enumerate(steps):
-        m = own_member() ^ step
-        k_ref, v_ref, out_ref = k_refs.at[n], v_refs.at[n], out_refs[n]
         bias = dead_slots(slots_ref[m, SLOTS])
         for g in range(GROUP):
             scores = scored(x_ref.at[m], g, k_ref) + bias
@@ -285,7 +280,13 @@
             keep = jnp.exp2((before - top) * EXP2_SCALE)
             total = mixed[:, HEAD_DIM:] + keep * sum_ref[m, g]
             mixed = mixed[:, :HEAD_DIM] + keep * mix_ref[m, g]
-            out_ref[:, g * HEAD_DIM : (g + 1) * HEAD_DIM] = (mixed / total).astype(jnp.bfloat16)
+            cols = slice(g * HEAD_DIM, (g + 1) * HEAD_DIM)
+            done_ref[n, :, cols] = (mixed / total).astype(jnp.bfloat16)
+        return carry
+
+    lax.fori_loop(0, len(out_refs), one, 0)
+    for n, out_ref in enumerate(out_refs):
+        out_ref[...] = done_ref[n]
 
 
 def head_kernel(alive_ref, x_ref, far_k_ref, far_v_ref, out_ref, k_ref, v_ref):
@@ -350,24 +351,26 @@
     far, running = lax.optimization_barrier((far, running))
     far_there = [lax.ppermute(part, "c", swap) for part in far]
     outs = {}
-    for steps in STEPS:
-        count = len(steps)
-        keys = SLOTS * HALF
+    keys = SLOTS * HALF
+    shape = (BLOCK, GROUP * HEAD_DIM)
+    for mask in (4, 0):
         results = pl.pallas_call(
-            functools.partial(second_kernel, steps),
-            out_shape=[jax.ShapeDtypeStruct((BLOCK, GROUP * HEAD_DIM), bf)] * count,
+            functools.partial(second_kernel, mask),
+            out_shape=[jax.ShapeDtypeStruct(shape, bf)] * 4,
             in_specs=[SMEM] + [VMEM] * (4 + 2 * GROUPS),
-            out_specs=[VMEM] * count,
+            out_specs=[VMEM] * 4,
             scratch_shapes=[
-                pltpu.VMEM((count, keys, HEAD_DIM), bf),
-                pltpu.VMEM((count, keys, 2 * HEAD_DIM), bf),
+                pltpu.VMEM((keys, HEAD_DIM), bf),
+                pltpu.VMEM((keys, 2 * HEAD_DIM), bf),
+                pltpu.VMEM((4,) + shape, bf),
             ],
             compiler_params=room(24),
             cost_estimate=pl.CostEstimate(
-                flops=1 << 29, bytes_accessed=1 << 20, transcendentals=1 << 19
+                flops=1 << 30, bytes_accessed=1 << 21, transcendentals=1 << 20
             ),
         )(slots, members, *running, *far, *far_there)
-        for step, out in zip(steps, results):
+        for n, out in enumerate(results):
+            step = mask ^ n
             pairs = [(m, m ^ step) for m in range(KV_HEADS)]
             outs[step] = lax.ppermute(out, HEAD_AXES, pairs) if step else out
     return [outs[step] for step in range(KV_HEADS)]
@@ -380,7 +383,7 @@
         in_specs=[VMEM] * KV_HEADS,
         out_specs=HBM,
         scratch_shapes=[pltpu.SemaphoreType.DMA((KV_HEADS,))],
-        compiler_params=room(8),
+        compiler_params=pltpu.CompilerParams(vmem_limit_bytes=67043328),
     )(*outs)
 
 

time: 115 us -> 115 us (level)
    pallas_call x4 -> x2, Pallas kernels: 15.2 us -> 13.9 us  [quick(): pl.pallas_call(functools.partial(second_kernel, mask), out_shape=[jax.Sha...]
    pallas_call x1, Pallas kernels: 1.11 us -> 2.31 us  [join(): pl.pallas_call(join_kernel, out_shape=jax.ShapeDtypeStruct((BLOCK, HEADS...]
    unnamed x20 -> x18, local copies, waits for them, and re-layouts: 4.57 us -> 3.6 us
  transfers between devices with their start and end apart: 22 -> 22, of which waited for: 7 -> 9; matrix products, arithmetic and copies ran while one was open for 0% -> 0% of each run, Pallas kernels for 24% -> 20%
where the time goes in v1:
time: 115 us; the launch traced here: 113 us
  starting transfers between devices  50 us (43%)
  Pallas kernels  34.9 us (30%)
  waiting for transfers between devices  23.7 us (21%)
  local copies, waits for them, and re-layouts  3.6 us (3%)
    all_to_all x1, starting transfers between devices, shards(): lax.all_to_all(send.reshape(DEVICES, 8, HEAD_DIM), AXES, 0, 0, tiled=True)  15.7 us
    pallas_call x2, Pallas kernels, quick(): pl.pallas_call(functools.partial(second_kernel, mask), out_shape=[jax.Sha...  13.9 us
    ppermute x7, starting transfers between devices, quick(): got[d] = lax.ppermute(packs[d], 'z', pairs)  11.6 us
    all_to_all x1, waiting for transfers between devices, shards(): lax.all_to_all(send.reshape(DEVICES, 8, HEAD_DIM), AXES, 0, 0, tiled=True)  11 us
    ppermute x7, starting transfers between devices, quick(): outs[step] = lax.ppermute(out, HEAD_AXES, pairs) if step else out  9.71 us
    pallas_call x1, Pallas kernels, quick(): pl.pallas_call(first_kernel, out_shape=(jax.ShapeDtypeStruct((KV_HEADS, G...  8.31 us
    ppermute x2, starting transfers between devices, quick(): near_there.append(lax.ppermute(part, 'c', swap))  5.47 us
    ppermute x2, waiting for transfers between devices, quick(): far.append(lax.ppermute(part, 'xh', swap))  4.28 us
  transfers between devices with their start and end apart: 22, of which 9 were waited for; matrix products, arithmetic and copies ran while one was open for 0% of the time, Pallas kernels for 20%

profile of v1, /device:TPU:1, one launch (start us, length us, event | category | flops | bytes accessed | tf_op | source)
XLA Modules:
  0.0 113.2 jit_solution(13087659339290165118)
XLA Ops:
  0.0 0.0 copy-start
  0.0 2.9 %shard_map.76 = (bf16[8,2,4,2,2,8,128]{6,5,4,3,2,1,0:T(8,128)(2,1)}, f32[128,128]{1,0:T(8,128)}, f32[128,128]{1,0:T(8,128)}, bf16[128,1024]{1,0:T(8,128)(2,1)}) custom-call(s32[32768]{0:T(1024)} %pos_ref.1, f32[1,128]{1,0:T(1,128)} %constant.46.clone.inv_ref, bf16[128,1024]{1,0:T(8,128)(2,1)} %k_hbm.1, bf16[128,1024]{1,0:T(8,128)(2,1)} %v_ref.1), custom_call_target="tpu_custom_call" | custom-call | tf_op jit(solution)/shard_map/pallas_call | solution.py:421
  2.9 15.7 %all-to-all-start.1 = ((bf16[256,8,128]{2,1,0:T(8,128)(2,1)}), bf16[256,8,128]{2,1,0:T(8,128)(2,1)S(1)}, u32[]{:S(2)}, u32[]{:S(2)}) async-start(bf16[256,8,128]{2,1,0:T(8,128)(2,1)} %bitcast.26), calls=%async_computation.1 | async-start | bytes 1048576 | tf_op jit(solution)/shard_map/all_to_all | solution.py:436
  18.5 2.1 %shard_map.75 = (s32[34,8]{1,0:T(8,128)S(1)}, s32[8,8]{1,0:T(8,128)S(1)}, s32[1,1]{1,0:T(1,128)}) custom-call(s32[256,128]{1,0:T(8,128)} %bitcast.27, s32[8,256]{1,0:T(8,128)} %bitcast.36), custom_call_target="tpu_custom_call" | custom-call | flops 4194304 | bytes 4194304 | tf_op jit(solution)/shard_map/pallas_call | solution.py:439
  20.6 0.0 copy-done
  20.6 0.0 copy-start.1
  20.6 0.9 copy-done.1
  21.6 0.9 copy-done.2
  22.5 0.8 copy-done.3
  23.4 0.8 copy-done.4
  24.2 4.2 %shard_map.77 = bf16[8,128,768]{2,1,0:T(8,128)(2,1)} custom-call(s32[1,1]{1,0:T(1,128)} %get-tuple-element.75.count_ref, f32[128,128]{1,0:T(8,128)S(1)} %copy-done.3, f32[128,128]{1,0:T(8,128)S(1)} %copy-done.4, bf16[128,4096]{1,0:T(8,128)(2,1)S(1)} %copy-done, bf16[128,1024]{1,0:T(8,128)(2,1)S(1)} %copy-done.2, bf16[128,1024]{1,0:T(8,128)(2,1)S(1)} %copy-done.1), custom_call_target="tpu_custom_call" | custom-call | flops 4194304 | bytes 4194304 | tf_op jit(solution)/shard_map/pallas_call | solution.py:450
  28.4 11.0 %all-to-all-done.1.src_ref = bf16[256,8,128]{2,1,0:T(8,128)(2,1)S(1)} async-done(((bf16[256,8,128]{2,1,0:T(8,128)(2,1)}), bf16[256,8,128]{2,1,0:T(8,128)(2,1)S(1)}, u32[]{:S(2)}, u32[]{:S(2)}) %all-to-all-start.1) | async-done | bytes 524320 | tf_op jit(solution)/shard_map/all_to_all | solution.py:436
  39.4 3.6 %all-to-all-start.2 = ((bf16[8,128,768]{2,1,0:T(8,128)(2,1)}), bf16[8,128,768]{2,1,0:T(8,128)(2,1)S(1)}, u32[]{:S(2)}, u32[]{:S(2)}) async-start(bf16[8,128,768]{2,1,0:T(8,128)(2,1)} %shard_map.77), calls=%async_computation.2 | async-start | bytes 3145728 | tf_op jit(solution)/shard_map/all_to_all | solution.py:459
  43.0 1.3 %shard_map.78 = (bf16[34,8,128]{2,1,0:T(8,128)(2,1)S(1)}, bf16[34,8,128]{2,1,0:T(8,128)(2,1)S(1)}, bf16[34,8,128]{2,1,0:T(8,128)(2,1)S(1)}, bf16[34,8,128]{2,1,0...) custom-call(s32[34,8]{1,0:T(8,128)S(1)} %get-tuple-element.81.picks_, ...), custom_call_target="tpu_custom_call" | custom-call | tf_op jit(solution)/shard_map/pallas_call | solution.py:315
  44.2 0.1 collective-permute-start.4
  44.3 2.8 %collective-permute-start.5 = (bf16[34,8,128]{2,1,0:T(8,128)(2,1)S(1)}, bf16[34,8,128]{2,1,0:T(8,128)(2,1)S(1)}, u32[]{:S(2)}, u32[]{:S(2)}) collective-permute-start(bf16[34,8,128]{2,1,0:T(8,128)(2,1)S(1)} %get-tuple-element.87), channel_id=1, source_target_pairs={{0,96},{32,128},{64,160},{96,192},{128,224},{160,0},{192,32},{224,... | collective-permute-start | bytes 208904 | tf_op jit(solution)/shard_map/ppermute | solution.py:327
  47.1 1.8 %collective-permute-start.6 = (bf16[34,8,128]{2,1,0:T(8,128)(2,1)S(1)}, bf16[34,8,128]{2,1,0:T(8,128)(2,1)S(1)}, u32[]{:S(2)}, u32[]{:S(2)}) collective-permute-start(bf16[34,8,128]{2,1,0:T(8,128)(2,1)S(1)} %get-tuple-element.88), channel_id=1, source_target_pairs={{0,160},{32,192},{64,224},{96,0},{128,32},{160,64},{192,96},{224,1... | collective-permute-start | bytes 208904 | tf_op jit(solution)/shard_map/ppermute | solution.py:327
  48.9 4.3 %collective-permute-start.7 = (bf16[34,8,128]{2,1,0:T(8,128)(2,1)S(1)}, bf16[34,8,128]{2,1,0:T(8,128)(2,1)S(1)}, u32[]{:S(2)}, u32[]{:S(2)}) collective-permute-start(bf16[34,8,128]{2,1,0:T(8,128)(2,1)S(1)} %get-tuple-element.89), channel_id=1, source_target_pairs={{0,128},{32,160},{64,192},{96,224},{128,0},{160,32},{192,64},{224,... | collective-permute-start | bytes 208904 | tf_op jit(solution)/shard_map/ppermute | solution.py:327
  53.2 0.0 collective-permute-start
  53.2 0.0 collective-permute-done.4
  53.2 2.7 %collective-permute-start.1 = (bf16[34,8,128]{2,1,0:T(8,128)(2,1)S(1)}, bf16[34,8,128]{2,1,0:T(8,128)(2,1)S(1)}, u32[]{:S(2)}, u32[]{:S(2)}) collective-permute-start(bf16[34,8,128]{2,1,0:T(8,128)(2,1)S(1)} %get-tuple-element.84), channel_id=1, source_target_pairs={{0,224},{32,0},{64,32},{96,64},{128,96},{160,128},{192,160},{224,1... | collective-permute-start | bytes 208904 | tf_op jit(solution)/shard_map/ppermute | solution.py:327
  55.8 0.0 collective-permute-done.5
  55.9 0.0 collective-permute-start.2
  55.9 0.0 collective-permute-done.6
  55.9 1.5 %collective-permute-done.7 = bf16[34,8,128]{2,1,0:T(8,128)(2,1)S(1)} collective-permute-done((bf16[34,8,128]{2,1,0:T(8,128)(2,1)S(1)}, bf16[34,8,128]{2,1,0:T(8,128)(2,1)S(1)}, u32[]{:S(2)}, u32[]{:S(2)}) %collective-permute-start.7) | collective-permute-done | bytes 69664 | tf_op jit(solution)/shard_map/ppermute | solution.py:327
  57.4 0.0 copy-done.5
  57.4 3.0 %collective-permute-start.10 = (bf16[34,32,128]{2,1,0:T(8,128)(2,1)S(1)}, bf16[34,32,128]{2,1,0:T(8,128)(2,1)S(1)}, u32[]{:S(2)}, u32[]{:S(2)}) collective-permute-start(bf16[34,32,128]{2,1,0:T(8,128)(2,1)S(1)} %copy_bitcast_fusion.refs_1_), channel_id=1, source_target_pairs={{0,16},{16,0},{1,17},{17,1},{2,18},{18,2},{3,19},{19,3},{4,20},{20... | collective-permute-start | bytes 835592 | tf_op jit(solution)/shard_map/ppermute | solution.py:336
  60.4 0.0 collective-permute-done
  60.4 0.0 collective-permute-done.1
  60.4 1.4 %collective-permute-done.2 = bf16[34,8,128]{2,1,0:T(8,128)(2,1)S(1)} collective-permute-done((bf16[34,8,128]{2,1,0:T(8,128)(2,1)S(1)}, bf16[34,8,128]{2,1,0:T(8,128)(2,1)S(1)}, u32[]{:S(2)}, u32[]{:S(2)}) %collective-permute-start.2) | collective-permute-done | bytes 69664 | tf_op jit(solution)/shard_map/ppermute | solution.py:327
  61.9 2.5 %collective-permute-start.9 = (bf16[34,32,128]{2,1,0:T(8,128)(2,1)S(1)}, bf16[34,32,128]{2,1,0:T(8,128)(2,1)S(1)}, u32[]{:S(2)}, u32[]{:S(2)}) collective-permute-start(bf16[34,32,128]{2,1,0:T(8,128)(2,1)S(1)} %copy_bitcast_fusion.1.refs_0_), channel_id=1, source_target_pairs={{0,16},{16,0},{1,17},{17,1},{2,18},{18,2},{3,19},{19,3},{4,20},{20... | collective-permute-start | bytes 835592 | tf_op jit(solution)/shard_map/ppermute | solution.py:336
  64.4 1.4 %collective-permute-start.8 = (bf16[34,32,128]{2,1,0:T(8,128)(2,1)S(1)}, bf16[34,32,128]{2,1,0:T(8,128)(2,1)S(1)}, u32[]{:S(2)}, u32[]{:S(2)}) collective-permute-start(bf16[34,32,128]{2,1,0:T(8,128)(2,1)S(1)} %copy_bitcast_fusion.refs_1_), channel_id=1, source_target_pairs={{0,2},{2,0},{1,3},{3,1},{4,6},{6,4},{5,7},{7,5},{8,10},{10,8},{9,1... | collective-permute-start | bytes 835592 | tf_op jit(solution)/shard_map/ppermute | solution.py:335
  65.7 1.6 %collective-permute-start.3 = (bf16[34,32,128]{2,1,0:T(8,128)(2,1)S(1)}, bf16[34,32,128]{2,1,0:T(8,128)(2,1)S(1)}, u32[]{:S(2)}, u32[]{:S(2)}) collective-permute-start(bf16[34,32,128]{2,1,0:T(8,128)(2,1)S(1)} %copy_bitcast_fusion.1.refs_0_), channel_id=1, source_target_pairs={{0,2},{2,0},{1,3},{3,1},{4,6},{6,4},{5,7},{7,5},{8,10},{10,8},{9,1... | collective-permute-start | bytes 835592 | tf_op jit(solution)/shard_map/ppermute | solution.py:335
  67.3 0.0 all-to-all-done.2.x_ref
  67.3 0.0 collective-permute-done.10.refs_3_
  67.3 0.0 collective-permute-done.9.refs_2_
  67.4 8.3 %shard_map.79 = (f32[8,4,128,128]{3,2,1,0:T(8,128)S(1)}, f32[8,4,128,1]{3,2,1,0:T(8,128)S(1)}, f32[8,4,128,1]{3,2,1,0:T(8,128)S(1)}) custom-call(s32[8,8]{1,0:T(8,128)S(1)} %get-tuple-element.80.slots_ref, bf16[8,128,768]{2,1,0:T(8,128)(2,1)S(1)} %all-to-all-done.2.x_ref, bf16[34,32,128]{2,1,0:T(8,128)(2,1)S(1)} %copy_bitcast_fusion.1.refs_0_, ...), custom_call_target="tpu_custom_call" | custom-call | flops 2147483648 | bytes 4194304 | tf_op jit(solution)/shard_map/pallas_call | solution.py:338
  75.7 0.0 collective-permute-done.8.refs_1_
  75.7 4.3 %collective-permute-done.3.refs_0_ = bf16[34,32,128]{2,1,0:T(8,128)(2,1)S(1)} collective-permute-done((bf16[34,32,128]{2,1,0:T(8,128)(2,1)S(1)}, bf16[34,32,128]{2,1,0:T(8,128)(2,1)S(1)}, u32[]{:S(2)}, u32[]{:S(2)}) %collective-permute-start.3) | collective-permute-done | bytes 278560 | tf_op jit(solution)/shard_map/ppermute | solution.py:335
  80.0 1.0 collective-permute-start.11
  80.9 0.0 collective-permute-start.12
  80.9 1.2 %collective-permute-done.11.refs_2_ = bf16[34,32,128]{2,1,0:T(8,128)(2,1)S(1)} collective-permute-done((bf16[34,32,128]{2,1,0:T(8,128)(2,1)S(1)}, bf16[34,32,128]{2,1,0:T(8,128)(2,1)S(1)}, u32[]{:S(2)}, u32[]{:S(2)}) %collective-permute-start.11) | collective-permute-done | bytes 278560 | tf_op jit(solution)/shard_map/ppermute | solution.py:352
  82.1 0.4 collective-permute-done.12.refs_3_
  82.5 6.6 %shard_map.81 = (bf16[128,512]{1,0:T(8,128)(2,1)S(1)}, bf16[128,512]{1,0:T(8,128)(2,1)S(1)}, bf16[128,512]{1,0:T(8,128)(2,1)S(1)}, bf16[128,512]{1,0:T(8,128)(2,1)S(1)}) custom-call(s32[8,8]{1,0:T(8,128)S(1)} %get-tuple-element.80.slots_ref, bf16[8,128,768]{2,1,0:T(8,128)(2,1)S(1)} %all-to-all-done.2.x_ref, ...), custom_call_target="tpu_custom_call" | custom-call | flops 1073741824 | bytes 2097152 | tf_op jit(solution)/shard_map/pallas_call | solution.py:357
  89.1 3.4 %collective-permute-start.16 = (bf16[128,512]{1,0:T(8,128)(2,1)S(1)}, bf16[128,512]{1,0:T(8,128)(2,1)}, u32[]{:S(2)}, u32[]{:S(2)}) collective-permute-start(bf16[128,512]{1,0:T(8,128)(2,1)S(1)} %get-tuple-element.102), channel_id=1, source_target_pairs={{0,8},{1,9},{4,12},{5,13},{8,0},{9,1},{12,4},{13,5},{2,10},{3,11},... | collective-permute-start | bytes 393224 | tf_op jit(solution)/shard_map/ppermute | solution.py:375
  92.5 1.2 %collective-permute-start.17 = (bf16[128,512]{1,0:T(8,128)(2,1)S(1)}, bf16[128,512]{1,0:T(8,128)(2,1)}, u32[]{:S(2)}, u32[]{:S(2)}) collective-permute-start(bf16[128,512]{1,0:T(8,128)(2,1)S(1)} %get-tuple-element.103), channel_id=1, source_target_pairs={{0,9},{1,8},{4,13},{5,12},{8,1},{9,0},{12,5},{13,4},{2,11},{3,10},... | collective-permute-start | bytes 393224 | tf_op jit(solution)/shard_map/ppermute | solution.py:375
  93.7 2.4 %collective-permute-start.18 = (bf16[128,512]{1,0:T(8,128)(2,1)S(1)}, bf16[128,512]{1,0:T(8,128)(2,1)}, u32[]{:S(2)}, u32[]{:S(2)}) collective-permute-start(bf16[128,512]{1,0:T(8,128)(2,1)S(1)} %get-tuple-element.104), channel_id=1, source_target_pairs={{0,12},{1,13},{4,8},{5,9},{8,4},{9,5},{12,0},{13,1},{2,14},{3,15},... | collective-permute-start | bytes 393224 | tf_op jit(solution)/shard_map/ppermute | solution.py:375
  96.1 0.1 collective-permute-start.19
  96.2 7.3 %shard_map.80 = (bf16[128,512]{1,0:T(8,128)(2,1)}, bf16[128,512]{1,0:T(8,128)(2,1)S(1)}, bf16[128,512]{1,0:T(8,128)(2,1)S(1)}, bf16[128,512]{1,0:T(8,128)(2,1)S(1)}) custom-call(s32[8,8]{1,0:T(8,128)S(1)} %get-tuple-element.80.slots_ref, bf16[8,128,768]{2,1,0:T(8,128)(2,1)S(1)} %all-to-all-done.2.x_ref, f32[8,4,128,128]{3,2,1,0:T(8,128)S(1)} %get-tuple-element.93.mix_ref, ...), custom_call_target="tpu_custom_call" | custom-call | flops 1073741824 | bytes 2097152 | tf_op jit(solution)/shard_map/pallas_call | solution.py:357
  103.4 1.3 %collective-permute-start.13 = (bf16[128,512]{1,0:T(8,128)(2,1)S(1)}, bf16[128,512]{1,0:T(8,128)(2,1)}, u32[]{:S(2)}, u32[]{:S(2)}) collective-permute-start(bf16[128,512]{1,0:T(8,128)(2,1)S(1)} %get-tuple-element.99), channel_id=1, source_target_pairs={{0,1},{1,0},{4,5},{5,4},{8,9},{9,8},{12,13},{13,12},{2,3},{3,2},{6... | collective-permute-start | bytes 393224 | tf_op jit(solution)/shard_map/ppermute | solution.py:375
  104.8 0.0 collective-permute-done.16
  104.8 0.0 collective-permute-start.14
  104.8 0.0 collective-permute-done.17
  104.8 1.3 %collective-permute-start.15 = (bf16[128,512]{1,0:T(8,128)(2,1)S(1)}, bf16[128,512]{1,0:T(8,128)(2,1)}, u32[]{:S(2)}, u32[]{:S(2)}) collective-permute-start(bf16[128,512]{1,0:T(8,128)(2,1)S(1)} %get-tuple-element.101), channel_id=1, source_target_pairs={{0,5},{1,4},{4,1},{5,0},{8,13},{9,12},{12,9},{13,8},{2,7},{3,6},{6... | collective-permute-start | bytes 393224 | tf_op jit(solution)/shard_map/ppermute | solution.py:375
  106.7 0.0 collective-permute-done.18
  106.8 0.0 collective-permute-done.19
  106.8 0.6 collective-permute-done.13
  107.4 2.0 %collective-permute-done.14 = bf16[128,512]{1,0:T(8,128)(2,1)} collective-permute-done((bf16[128,512]{1,0:T(8,128)(2,1)S(1)}, bf16[128,512]{1,0:T(8,128)(2,1)}, u32[]{:S(2)}, u32[]{:S(2)}) %collective-permute-start.14) | collective-permute-done | bytes 131104 | tf_op jit(solution)/shard_map/ppermute | solution.py:375
  109.4 1.3 %collective-permute-done.15 = bf16[128,512]{1,0:T(8,128)(2,1)} collective-permute-done((bf16[128,512]{1,0:T(8,128)(2,1)S(1)}, bf16[128,512]{1,0:T(8,128)(2,1)}, u32[]{:S(2)}, u32[]{:S(2)}) %collective-permute-start.15) | collective-permute-done | bytes 131104 | tf_op jit(solution)/shard_map/ppermute | solution.py:375
  110.7 0.0 copy-done.6
  110.7 0.0 copy-done.7
  110.7 0.0 copy-done.8
  110.7 2.3 %conditional.1 = (bf16[128,4096]{1,0:T(8,128)(2,1)}) conditional(s32[]{:T(128)} %bitcast.8, (s32[32768]{0:T(1024)S(1)}, s32[256,8]{0,1:T(8,128)S(1)}, bf16[256,8,128]{2,1,0:T(8,128)(2,1)S(1)}, bf16[8,128,768]{2,1,0:T(8,128)(2,1)}) %tuple.27, (bf16[128,512]{1,0:T(8,128)(2,1)}, bf16[128,512]{1,0:T(8,128)(2,1)}, bf16[128,512]{1,0:T(8,128)(2,1)}, ...), branch_computations={%region_0.3_spmd, %region_3.4_spmd} | conditional | flops 208409 | bytes 18487626 | solution.py:462
  110.7 2.3 %branch_1_fun.1 = bf16[128,4096]{1,0:T(8,128)(2,1)} custom-call(bf16[128,512]{1,0:T(8,128)(2,1)} %get-tuple-element.36.refs_0_, bf16[128,512]{1,0:T(8,128)(2,1)} %get-tuple-element.37.refs_1_, bf16[128,512]{1,0:T(8,128)(2,1)} %get-tuple-element.38.refs_2_, bf16[128,512]{1,0:T(8,128)(2,1)} %get-tuple-element.39.refs_3_, ...), custom_call_target="tpu_custom_call" | custom-call | tf_op jit(solution)/shard_map/cond/branch_1_fun/pallas_call | solution.py:380
  (9 shorter events, 0.1 us)
Async XLA Ops:
  0.0 20.6 %copy-start = (bf16[128,4096]{1,0:T(8,128)(2,1)S(1)}, bf16[128,4096]{1,0:T(8,128)(2,1)}, u32[]{:S(2)}) copy-start(bf16[128,4096]{1,0:T(8,128)(2,1)} %q_ref.1) | copy-start | bytes 3145732
  2.9 36.5 %all-to-all-start.1 = ((bf16[256,8,128]{2,1,0:T(8,128)(2,1)}), bf16[256,8,128]{2,1,0:T(8,128)(2,1)S(1)}, u32[]{:S(2)}, u32[]{:S(2)}) async-start(bf16[256,8,128]{2,1,0:T(8,128)(2,1)} %bitcast.26), calls=%async_computation.1 | async-start | bytes 1048576 | tf_op jit(solution)/shard_map/all_to_all | solution.py:436
  20.6 1.0 copy-start.1
  21.6 0.9 copy-start.2
  22.5 0.8 copy-start.3
  23.4 0.8 copy-start.4
  39.4 18.1 %copy-start.5 = (bf16[256,8,128]{2,1,0:T(8,128)(2,1)}, bf16[256,8,128]{2,1,0:T(8,128)(2,1)S(1)}, u32[]{:S(2)}) copy-start(bf16[256,8,128]{2,1,0:T(8,128)(2,1)S(1)} %all-to-all-done.1.src_ref) | copy-start | bytes 1572868
  39.4 28.0 %all-to-all-start.2 = ((bf16[8,128,768]{2,1,0:T(8,128)(2,1)}), bf16[8,128,768]{2,1,0:T(8,128)(2,1)S(1)}, u32[]{:S(2)}, u32[]{:S(2)}) async-start(bf16[8,128,768]{2,1,0:T(8,128)(2,1)} %shard_map.77), calls=%async_computation.2 | async-start | bytes 3145728 | tf_op jit(solution)/shard_map/all_to_all | solution.py:459
  44.2 9.0 %collective-permute-start.4 = (bf16[34,8,128]{2,1,0:T(8,128)(2,1)S(1)}, bf16[34,8,128]{2,1,0:T(8,128)(2,1)S(1)}, u32[]{:S(2)}, u32[]{:S(2)}) collective-permute-start(bf16[34,8,128]{2,1,0:T(8,128)(2,1)S(1)} %get-tuple-element.86), channel_id=1, source_target_pairs={{0,192},{32,224},{64,0},{96,32},{128,64},{160,96},{192,128},{224,1... | collective-permute-start | bytes 208904 | tf_op jit(solution)/shard_map/ppermute | solution.py:327
  44.3 11.5 %collective-permute-start.5 = (bf16[34,8,128]{2,1,0:T(8,128)(2,1)S(1)}, bf16[34,8,128]{2,1,0:T(8,128)(2,1)S(1)}, u32[]{:S(2)}, u32[]{:S(2)}) collective-permute-start(bf16[34,8,128]{2,1,0:T(8,128)(2,1)S(1)} %get-tuple-element.87), channel_id=1, source_target_pairs={{0,96},{32,128},{64,160},{96,192},{128,224},{160,0},{192,32},{224,... | collective-permute-start | bytes 208904 | tf_op jit(solution)/shard_map/ppermute | solution.py:327
  47.1 8.8 %collective-permute-start.6 = (bf16[34,8,128]{2,1,0:T(8,128)(2,1)S(1)}, bf16[34,8,128]{2,1,0:T(8,128)(2,1)S(1)}, u32[]{:S(2)}, u32[]{:S(2)}) collective-permute-start(bf16[34,8,128]{2,1,0:T(8,128)(2,1)S(1)} %get-tuple-element.88), channel_id=1, source_target_pairs={{0,160},{32,192},{64,224},{96,0},{128,32},{160,64},{192,96},{224,1... | collective-permute-start | bytes 208904 | tf_op jit(solution)/shard_map/ppermute | solution.py:327
  48.9 8.5 %collective-permute-start.7 = (bf16[34,8,128]{2,1,0:T(8,128)(2,1)S(1)}, bf16[34,8,128]{2,1,0:T(8,128)(2,1)S(1)}, u32[]{:S(2)}, u32[]{:S(2)}) collective-permute-start(bf16[34,8,128]{2,1,0:T(8,128)(2,1)S(1)} %get-tuple-element.89), channel_id=1, source_target_pairs={{0,128},{32,160},{64,192},{96,224},{128,0},{160,32},{192,64},{224,... | collective-permute-start | bytes 208904 | tf_op jit(solution)/shard_map/ppermute | solution.py:327
  53.2 7.3 %collective-permute-start = (bf16[34,8,128]{2,1,0:T(8,128)(2,1)S(1)}, bf16[34,8,128]{2,1,0:T(8,128)(2,1)S(1)}, u32[]{:S(2)}, u32[]{:S(2)}) collective-permute-start(bf16[34,8,128]{2,1,0:T(8,128)(2,1)S(1)} %get-tuple-element.83), channel_id=1, source_target_pairs={{0,32},{32,64},{64,96},{96,128},{128,160},{160,192},{192,224},{224... | collective-permute-start | bytes 208904 | tf_op jit(solution)/shard_map/ppermute | solution.py:327
  53.2 7.2 %collective-permute-start.1 = (bf16[34,8,128]{2,1,0:T(8,128)(2,1)S(1)}, bf16[34,8,128]{2,1,0:T(8,128)(2,1)S(1)}, u32[]{:S(2)}, u32[]{:S(2)}) collective-permute-start(bf16[34,8,128]{2,1,0:T(8,128)(2,1)S(1)} %get-tuple-element.84), channel_id=1, source_target_pairs={{0,224},{32,0},{64,32},{96,64},{128,96},{160,128},{192,160},{224,1... | collective-permute-start | bytes 208904 | tf_op jit(solution)/shard_map/ppermute | solution.py:327
  55.9 6.0 %collective-permute-start.2 = (bf16[34,8,128]{2,1,0:T(8,128)(2,1)S(1)}, bf16[34,8,128]{2,1,0:T(8,128)(2,1)S(1)}, u32[]{:S(2)}, u32[]{:S(2)}) collective-permute-start(bf16[34,8,128]{2,1,0:T(8,128)(2,1)S(1)} %get-tuple-element.85), channel_id=1, source_target_pairs={{0,64},{32,96},{64,128},{96,160},{128,192},{160,224},{192,0},{224,... | collective-permute-start | bytes 208904 | tf_op jit(solution)/shard_map/ppermute | solution.py:327
  57.4 9.9 %collective-permute-start.10 = (bf16[34,32,128]{2,1,0:T(8,128)(2,1)S(1)}, bf16[34,32,128]{2,1,0:T(8,128)(2,1)S(1)}, u32[]{:S(2)}, u32[]{:S(2)}) collective-permute-start(bf16[34,32,128]{2,1,0:T(8,128)(2,1)S(1)} %copy_bitcast_fusion.refs_1_), channel_id=1, source_target_pairs={{0,16},{16,0},{1,17},{17,1},{2,18},{18,2},{3,19},{19,3},{4,20},{20... | collective-permute-start | bytes 835592 | tf_op jit(solution)/shard_map/ppermute | solution.py:336
  61.9 5.5 %collective-permute-start.9 = (bf16[34,32,128]{2,1,0:T(8,128)(2,1)S(1)}, bf16[34,32,128]{2,1,0:T(8,128)(2,1)S(1)}, u32[]{:S(2)}, u32[]{:S(2)}) collective-permute-start(bf16[34,32,128]{2,1,0:T(8,128)(2,1)S(1)} %copy_bitcast_fusion.1.refs_0_), channel_id=1, source_target_pairs={{0,16},{16,0},{1,17},{17,1},{2,18},{18,2},{3,19},{19,3},{4,20},{20... | collective-permute-start | bytes 835592 | tf_op jit(solution)/shard_map/ppermute | solution.py:336
  64.4 11.3 %collective-permute-start.8 = (bf16[34,32,128]{2,1,0:T(8,128)(2,1)S(1)}, bf16[34,32,128]{2,1,0:T(8,128)(2,1)S(1)}, u32[]{:S(2)}, u32[]{:S(2)}) collective-permute-start(bf16[34,32,128]{2,1,0:T(8,128)(2,1)S(1)} %copy_bitcast_fusion.refs_1_), channel_id=1, source_target_pairs={{0,2},{2,0},{1,3},{3,1},{4,6},{6,4},{5,7},{7,5},{8,10},{10,8},{9,1... | collective-permute-start | bytes 835592 | tf_op jit(solution)/shard_map/ppermute | solution.py:335
  65.7 14.2 %collective-permute-start.3 = (bf16[34,32,128]{2,1,0:T(8,128)(2,1)S(1)}, bf16[34,32,128]{2,1,0:T(8,128)(2,1)S(1)}, u32[]{:S(2)}, u32[]{:S(2)}) collective-permute-start(bf16[34,32,128]{2,1,0:T(8,128)(2,1)S(1)} %copy_bitcast_fusion.1.refs_0_), channel_id=1, source_target_pairs={{0,2},{2,0},{1,3},{3,1},{4,6},{6,4},{5,7},{7,5},{8,10},{10,8},{9,1... | collective-permute-start | bytes 835592 | tf_op jit(solution)/shard_map/ppermute | solution.py:335
  80.0 2.1 %collective-permute-start.11 = (bf16[34,32,128]{2,1,0:T(8,128)(2,1)S(1)}, bf16[34,32,128]{2,1,0:T(8,128)(2,1)S(1)}, u32[]{:S(2)}, u32[]{:S(2)}) collective-permute-start(bf16[34,32,128]{2,1,0:T(8,128)(2,1)S(1)} %collective-permute-done.3.refs_0_), channel_id=1, source_target_pairs={{0,16},{16,0},{1,17},{17,1},{2,18},{18,2},{3,19},{19,3},{4,20},{20... | collective-permute-start | bytes 835592 | tf_op jit(solution)/shard_map/ppermute | solution.py:352
  80.9 1.6 %collective-permute-start.12 = (bf16[34,32,128]{2,1,0:T(8,128)(2,1)S(1)}, bf16[34,32,128]{2,1,0:T(8,128)(2,1)S(1)}, u32[]{:S(2)}, u32[]{:S(2)}) collective-permute-start(bf16[34,32,128]{2,1,0:T(8,128)(2,1)S(1)} %collective-permute-done.8.refs_1_), channel_id=1, source_target_pairs={{0,16},{16,0},{1,17},{17,1},{2,18},{18,2},{3,19},{19,3},{4,20},{20... | collective-permute-start | bytes 835592 | tf_op jit(solution)/shard_map/ppermute | solution.py:352
  89.1 15.7 %collective-permute-start.16 = (bf16[128,512]{1,0:T(8,128)(2,1)S(1)}, bf16[128,512]{1,0:T(8,128)(2,1)}, u32[]{:S(2)}, u32[]{:S(2)}) collective-permute-start(bf16[128,512]{1,0:T(8,128)(2,1)S(1)} %get-tuple-element.102), channel_id=1, source_target_pairs={{0,8},{1,9},{4,12},{5,13},{8,0},{9,1},{12,4},{13,5},{2,10},{3,11},... | collective-permute-start | bytes 393224 | tf_op jit(solution)/shard_map/ppermute | solution.py:375
  92.5 12.3 %collective-permute-start.17 = (bf16[128,512]{1,0:T(8,128)(2,1)S(1)}, bf16[128,512]{1,0:T(8,128)(2,1)}, u32[]{:S(2)}, u32[]{:S(2)}) collective-permute-start(bf16[128,512]{1,0:T(8,128)(2,1)S(1)} %get-tuple-element.103), channel_id=1, source_target_pairs={{0,9},{1,8},{4,13},{5,12},{8,1},{9,0},{12,5},{13,4},{2,11},{3,10},... | collective-permute-start | bytes 393224 | tf_op jit(solution)/shard_map/ppermute | solution.py:375
  93.7 13.1 %collective-permute-start.18 = (bf16[128,512]{1,0:T(8,128)(2,1)S(1)}, bf16[128,512]{1,0:T(8,128)(2,1)}, u32[]{:S(2)}, u32[]{:S(2)}) collective-permute-start(bf16[128,512]{1,0:T(8,128)(2,1)S(1)} %get-tuple-element.104), channel_id=1, source_target_pairs={{0,12},{1,13},{4,8},{5,9},{8,4},{9,5},{12,0},{13,1},{2,14},{3,15},... | collective-permute-start | bytes 393224 | tf_op jit(solution)/shard_map/ppermute | solution.py:375
  96.1 14.6 %copy-start.6 = (bf16[256,8,128]{2,1,0:T(8,128)(2,1)S(1)}, bf16[256,8,128]{2,1,0:T(8,128)(2,1)}, u32[]{:S(2)}) copy-start(bf16[256,8,128]{2,1,0:T(8,128)(2,1)} %copy-done.5) | copy-start | bytes 1572868
  96.1 14.6 %copy-start.7 = (s32[32768]{0:T(1024)S(1)}, s32[32768]{0:T(1024)}, u32[]{:S(2)}) copy-start(s32[32768]{0:T(1024)} %param.13) | copy-start | bytes 393220
  96.1 14.6 %copy-start.8 = (s32[256,8]{0,1:T(8,128)S(1)}, s32[256,8]{0,1:T(8,128)}, u32[]{:S(2)}) copy-start(s32[256,8]{0,1:T(8,128)} %param.12) | copy-start | bytes 24580
  96.1 10.7 %collective-permute-start.19 = (bf16[128,512]{1,0:T(8,128)(2,1)S(1)}, bf16[128,512]{1,0:T(8,128)(2,1)}, u32[]{:S(2)}, u32[]{:S(2)}) collective-permute-start(bf16[128,512]{1,0:T(8,128)(2,1)S(1)} %get-tuple-element.105), channel_id=1, source_target_pairs={{0,13},{1,12},{4,9},{5,8},{8,5},{9,4},{12,1},{13,0},{2,15},{3,14},... | collective-permute-start | bytes 393224 | tf_op jit(solution)/shard_map/ppermute | solution.py:375
  103.4 3.9 %collective-permute-start.13 = (bf16[128,512]{1,0:T(8,128)(2,1)S(1)}, bf16[128,512]{1,0:T(8,128)(2,1)}, u32[]{:S(2)}, u32[]{:S(2)}) collective-permute-start(bf16[128,512]{1,0:T(8,128)(2,1)S(1)} %get-tuple-element.99), channel_id=1, source_target_pairs={{0,1},{1,0},{4,5},{5,4},{8,9},{9,8},{12,13},{13,12},{2,3},{3,2},{6... | collective-permute-start | bytes 393224 | tf_op jit(solution)/shard_map/ppermute | solution.py:375
  104.8 4.6 %collective-permute-start.14 = (bf16[128,512]{1,0:T(8,128)(2,1)S(1)}, bf16[128,512]{1,0:T(8,128)(2,1)}, u32[]{:S(2)}, u32[]{:S(2)}) collective-permute-start(bf16[128,512]{1,0:T(8,128)(2,1)S(1)} %get-tuple-element.100), channel_id=1, source_target_pairs={{0,4},{1,5},{4,0},{5,1},{8,12},{9,13},{12,8},{13,9},{2,6},{3,7},{6... | collective-permute-start | bytes 393224 | tf_op jit(solution)/shard_map/ppermute | solution.py:375
  104.8 5.9 %collective-permute-start.15 = (bf16[128,512]{1,0:T(8,128)(2,1)S(1)}, bf16[128,512]{1,0:T(8,128)(2,1)}, u32[]{:S(2)}, u32[]{:S(2)}) collective-permute-start(bf16[128,512]{1,0:T(8,128)(2,1)S(1)} %get-tuple-element.101), channel_id=1, source_target_pairs={{0,5},{1,4},{4,1},{5,0},{8,13},{9,12},{12,9},{13,8},{2,7},{3,6},{6... | collective-permute-start | bytes 393224 | tf_op jit(solution)/shard_map/ppermute | solution.py:375
